TPU v7x, 256 devices: a whole 4x4x8 slice. The times are simulated.
256 devices in a mesh: dp: 4 (over x), space: 64 (over z, y, core).
Axes of the slice: x: 4, y: 4, z: 8, core: 2. Of those that a mesh axis runs over, the one named last changes fastest.
Arguments:
- fields: bfloat16 [4, 32, 6144, 128], P('dp', None, 'space'), may hold values from -6 to 6
- land_mask: int32 [6144, 128], P('space'), may hold values from 0 to 1, as said below
- land_frac: float32 [6144, 128], P('space'), may hold values from 0.05 to 1
- owner_map: int32 [12288], replicated, may hold values from 0 to 12287, as said below
- targets: float32 [4, 14, 12288], P('dp', None, 'space'), may hold values from -3 to 3
- conv_weight: bfloat16 [3, 3, 32, 128], replicated, may hold values from -0.375 to 0.375
- conv_bias: float32 [128], replicated, may hold values from -3 to 3
- mix_weight: bfloat16 [128, 128], replicated, may hold values from -0.5 to 0.5
- mix_bias: float32 [128], replicated, may hold values from -3 to 3
- out_weight: bfloat16 [128, 14], replicated, may hold values from -0.5 to 0.5
- out_bias: float32 [14], replicated, may hold values from -3 to 3
Outputs:
- coarse_pred: float32 [4, 14, 12288], P('dp', None, 'space')
- conv_grad: float32 [3, 3, 32, 128], replicated
- conv_bias_grad: float32 [128], replicated
- mix_grad: float32 [128, 128], replicated
- mix_bias_grad: float32 [128], replicated
- out_grad: float32 [128, 14], replicated
- out_bias_grad: float32 [14], replicated
- loss: float32 [], replicated
Inputs may be any that keep to these rules, and one draw needn't show every extreme that they name: A permutation. Coarse cell g is owned by index owner_map[g] // 192 of space, at local place owner_map[g] % 192; the 192 coarse cells of every strip go to every owner exactly 3 at a time. `land_mask`: 1 marks land.
All inputs are finite; a program needn't handle non-finite values.
Results may differ from a plain program's by a relative error of at most 0.00039.
Values may be sent and summed in bfloat16 or wider, within the bound.
A program may use at most 128 MiB of HBM per device.

v0:
```python
import math

import jax
import jax.numpy as jnp
from jax import lax
from jax.sharding import PartitionSpec as P

SIDE = 8


CUBIC = 0.044715
ROOT_TWO_PI = math.sqrt(2.0 / math.pi)


def padded_2(block, sides, width):
    for axis, dim in sides:
        count = lax.axis_size(axis)
        forward = [(i, i + 1) for i in range(count - 1)]
        backward = [(target, source) for source, target in forward]
        low = lax.ppermute(
            lax.slice_in_dim(block, block.shape[dim] - width, None, axis=dim), axis, forward
        )
        high = lax.ppermute(lax.slice_in_dim(block, 0, width, axis=dim), axis, backward)
        block = jnp.concatenate([low, block, high], axis=dim)
    return block


def gelu_pair(pre):
    inner = ROOT_TWO_PI * (pre + CUBIC * pre * pre * pre)
    tanh_value = jnp.tanh(inner)
    value = 0.5 * pre * (1.0 + tanh_value)
    slope = 0.5 * (1.0 + tanh_value) + 0.5 * pre * (1.0 - tanh_value * tanh_value) * ROOT_TWO_PI * (
        1.0 + 3.0 * CUBIC * pre * pre
    )
    return (value, slope)


def product(form, left, right):
    return jnp.einsum(form, left, right, preferred_element_type=jnp.float32)


def block_sums(values, side):
    leading = values.shape[:-2]
    height, breadth = (values.shape[-2], values.shape[-1])
    shaped = values.reshape(leading + (height // side, side, breadth // side, side))
    return jnp.sum(shaped, axis=(-3, -1)).reshape(leading + (height // side * (breadth // side),))


def forward_tile(padded, conv_weight, conv_bias, mix_weight, mix_bias, out_weight, out_bias):
    height = padded.shape[2] - 2
    breadth = padded.shape[3] - 2
    pieces = [
        padded[:, :, row_shift : row_shift + height, col_shift : col_shift + breadth]
        for row_shift in range(3)
        for col_shift in range(3)
    ]
    stacked = jnp.concatenate(pieces, axis=1)
    flat_weight = conv_weight.reshape(-1, conv_weight.shape[3])
    pre_one = product("mkrc,kh->mrch", stacked, flat_weight) + conv_bias
    value_one, slope_one = gelu_pair(pre_one)
    hidden_one = value_one.astype(jnp.bfloat16)
    pre_two = product("mrch,hg->mrcg", hidden_one, mix_weight) + mix_bias
    value_two, slope_two = gelu_pair(pre_two)
    hidden_two = value_two.astype(jnp.bfloat16)
    raw = product("mrch,hp->mprc", hidden_two, out_weight) + out_bias[None, :, None, None]
    return (stacked, slope_one, hidden_one, slope_two, hidden_two, raw)


def backward_tile(
    stacked,
    slope_one,
    hidden_one,
    slope_two,
    hidden_two,
    raw,
    weight_map,
    d_block,
    mix_weight,
    out_weight,
    side,
):
    members, pools = (d_block.shape[0], d_block.shape[1])
    height, breadth = weight_map.shape
    d_cells = d_block.reshape(members, pools, height // side, breadth // side)
    d_cells = jnp.repeat(jnp.repeat(d_cells, side, axis=2), side, axis=3)
    d_raw = (d_cells * weight_map * jax.nn.sigmoid(raw)).astype(jnp.bfloat16)
    out_grad = product("mrch,mprc->hp", hidden_two, d_raw)
    out_bias_grad = jnp.sum(d_raw.astype(jnp.float32), axis=(0, 2, 3))
    d_two = (product("mprc,hp->mrch", d_raw, out_weight) * slope_two).astype(jnp.bfloat16)
    mix_grad = product("mrch,mrcg->hg", hidden_one, d_two)
    mix_bias_grad = jnp.sum(d_two.astype(jnp.float32), axis=(0, 1, 2))
    d_one = (product("mrcg,hg->mrch", d_two, mix_weight) * slope_one).astype(jnp.bfloat16)
    conv_grad = product("mkrc,mrch->kh", stacked, d_one)
    conv_bias_grad = jnp.sum(d_one.astype(jnp.float32), axis=(0, 1, 2))
    return (conv_grad, conv_bias_grad, mix_grad, mix_bias_grad, out_grad, out_bias_grad)


def route_tables(owner_map, position, peers, blocks):
    capacity = blocks // peers
    serial = jnp.arange(blocks, dtype=jnp.int32)
    owned = lax.dynamic_slice_in_dim(owner_map, position * blocks, blocks)
    target = owned // blocks
    earlier = serial[None, :] < serial[:, None]
    ranking = jnp.sum((target[None, :] == target[:, None]) & earlier, axis=1)
    send_slot = target * capacity + ranking
    slot_block = jnp.zeros((blocks,), jnp.int32).at[send_slot].set(serial)
    count_all = owner_map.shape[0]
    inverse = (
        jnp.zeros((count_all,), jnp.int32).at[owner_map].set(jnp.arange(count_all, dtype=jnp.int32))
    )
    mine_list = lax.dynamic_slice_in_dim(inverse, position * blocks, blocks)
    source = mine_list // blocks
    within = mine_list % blocks
    source_rows = owner_map.reshape(peers, blocks)[source] // blocks
    before = serial[None, :] < within[:, None]
    home_rank = jnp.sum((source_rows == position) & before, axis=1)
    home_slot = source * capacity + home_rank
    return (owned, send_slot, slot_block, home_slot, mine_list)


def on_device(
    fields,
    land_mask,
    land_frac,
    owner_map,
    targets,
    conv_weight,
    conv_bias,
    mix_weight,
    mix_bias,
    out_weight,
    out_bias,
):
    peers = lax.axis_size("space")
    position = lax.axis_index("space")
    members = fields.shape[0]
    pools = out_weight.shape[1]
    tile_rows = fields.shape[2]
    tile_cols = fields.shape[3]
    blocks = tile_rows // SIDE * (tile_cols // SIDE)
    capacity = blocks // peers
    extended = padded_2(fields, (("space", 2),), 1)
    padded = jnp.pad(extended, ((0, 0), (0, 0), (0, 0), (1, 1)))
    outputs = forward_tile(
        padded, conv_weight, conv_bias, mix_weight, mix_bias, out_weight, out_bias
    )
    weight_map = land_frac * land_mask.astype(jnp.float32)
    density = jax.nn.softplus(outputs[5]) * weight_map
    owned, send_slot, slot_block, home_slot, mine_list = route_tables(
        owner_map, position, peers, blocks
    )
    strip_values = block_sums(density, SIDE)
    strip_weights = block_sums(weight_map, SIDE)
    got_values, got_weights = (
        lax.all_to_all(
            strip_values[:, :, slot_block].reshape(members, pools, peers, capacity),
            "space",
            split_axis=2,
            concat_axis=2,
            tiled=True,
        ),
        lax.all_to_all(
            strip_weights[slot_block].reshape(1, 1, peers, capacity),
            "space",
            split_axis=2,
            concat_axis=2,
            tiled=True,
        ),
    )
    coarse_sum = got_values.reshape(members, pools, blocks)[:, :, home_slot]
    coarse_weight = got_weights.reshape(blocks)[home_slot]
    denom = jnp.maximum(coarse_weight, 1.0)
    coarse_pred = coarse_sum / denom
    residual = coarse_pred - targets
    count_all = members * lax.axis_size("dp") * pools * owner_map.shape[0]
    d_coarse = residual / (math.sqrt(count_all) * denom)
    serial = jnp.arange(blocks, dtype=jnp.int32)
    back_order = jnp.zeros((blocks,), jnp.int32).at[home_slot].set(serial)
    returned = lax.all_to_all(
        d_coarse[:, :, back_order].reshape(members, pools, peers, capacity),
        "space",
        split_axis=2,
        concat_axis=2,
        tiled=True,
    )
    d_block = returned.reshape(members, pools, blocks)[:, :, send_slot]
    grads = backward_tile(*outputs, weight_map, d_block, mix_weight, out_weight, SIDE)
    squares = jnp.sum(residual * residual)
    conv_grad, conv_bias_grad, mix_grad, mix_bias_grad, out_grad, out_bias_grad, total = lax.psum(
        (grads[0], grads[1], grads[2], grads[3], grads[4], grads[5], squares), ("dp", "space")
    )
    loss = 0.5 * total / count_all
    conv_grad = conv_grad.reshape(conv_weight.shape)
    return (
        coarse_pred,
        conv_grad,
        conv_bias_grad,
        mix_grad,
        mix_bias_grad,
        out_grad,
        out_bias_grad,
        loss,
    )


def solution(mesh):
    placed = (
        P("dp", None, "space", None),
        P("space", None),
        P("space", None),
        P(),
        P("dp", None, "space"),
        P(),
        P(),
        P(),
        P(),
        P(),
        P(),
    )
    return jax.shard_map(
        on_device,
        mesh=mesh,
        in_specs=placed,
        out_specs=(P("dp", None, "space"), P(), P(), P(), P(), P(), P(), P()),
        check_vma=False,
    )
```

profile of v0, /device:TPU:1, one launch (start us, length us, event | category | flops | bytes accessed | tf_op | source)
XLA Modules:
  0.0 443.7 jit_solution(1950870400691555517)
XLA Ops:
  8.7 4.6 %collective-permute-start = (bf16[1,32,1,128]{3,1,2,0:T(8,128)(2,1)S(1)}, bf16[1,32,1,128]{3,1,2,0:T(8,128)(2,1)S(1)}, u32[]{:S(2)}, u32[]{:S(2)}) collective-permute-start(bf16[1,32,1,128]{3,1,2,0:T(8,128)(2,1)S(1)} %get-tuple-element.61), channel_id=1, source_target_pairs={{0,1},{1,2},{2,3},{3,4},{4,5},{5,6},{6,7},{7,8},{8,9},{9,10},{10,1... | collective-permute-start | bytes 24584 | tf_op jit(solution)/shard_map/ppermute | solution.py:20
  13.3 1.9 collective-permute-start.1
  16.0 45.4 %scatter_custom_fusion.1 = s32[12288]{0:T(1024)S(1)} fusion(s32[12288]{0:T(1024)S(1)} %compare_select_fusion.1, s32[12288]{0:T(1024)S(1)} %iota.16, s32[]{:T(128)} %constant.30.clone.1), kind=kCustom, calls=%fused_computation.83 | custom fusion | bytes 49156 | tf_op jit(solution)/shard_map/scatter | solution.py:109
  67.6 12.9 %all-to-all-start.1 = ((f32[1,1,64,3]{3,1,0,2:T(1,128)}), f32[1,1,64,3]{3,1,0,2:T(1,128)S(1)}, u32[]{:S(2)}, u32[]{:S(2)}) async-start(f32[1,1,64,3]{3,1,0,2:T(1,128)} %bitcast.12), calls=%async_computation.1 | async-start | bytes 65536 | tf_op jit(solution)/shard_map/all_to_all | solution.py:162
  84.0 5.7 %all-to-all-done.1 = f32[1,1,64,3]{3,1,0,2:T(1,128)S(1)} async-done(((f32[1,1,64,3]{3,1,0,2:T(1,128)}), f32[1,1,64,3]{3,1,0,2:T(1,128)S(1)}, u32[]{:S(2)}, u32[]{:S(2)}) %all-to-all-start.1) | async-done | bytes 800 | tf_op jit(solution)/shard_map/all_to_all | solution.py:162
  96.1 2.9 copy-done.1
  99.0 2.7 fusion.2
  101.8 6.2 %multiply_convert_fusion = (bf16[96,128,128]{2,1,0:T(8,128)(2,1)S(1)}, f32[96,128,128]{2,1,0:T(8,128)}) fusion(f32[128]{0:T(128)S(1)} %copy-done.9, bf16[128,128]{1,0:T(8,128)(2,1)S(1)} %copy-done.8, f32[96,128,128]{2,1,0:T(8,128)S(1)} %fusion.2, f32[128]{0:T(128)S(1)} %copy-done.10), kind=kOutput, calls=%fused_computation.34 | convolution fusion | flops 434110464 | bytes 15762432 | tf_op jit(solution)/shard_map/mrch,hg->mrcg/dot_general | solution.py:39
  108.0 1.8 fusion.25
  110.9 8.5 %reshape.223 = f32[14,12,8,16,8]{4,3,2,1,0:T(8,128)} reshape(f32[14,96,128]{2,1,0:T(8,128)} %copy.77) | data formatting | bytes 1376256 | tf_op jit(solution)/shard_map/reshape | solution.py:45
  119.4 5.6 %reduce_sum.72 = f32[14,12,16]{2,1,0:T(8,128)} reduce(f32[14,12,8,16,8]{4,3,2,1,0:T(8,128)} %reshape.223, f32[]{:T(128)} %constant.29.clone.1), dimensions={2,4}, to_apply=%region_0.1 | reduce | flops 169344 | bytes 698884 | tf_op jit(solution)/shard_map/reduce_sum | solution.py:46
  127.3 4.7 %all-to-all-start = ((f32[1,14,64,3]{1,0,3,2:T(1,128)}), f32[1,14,64,3]{1,0,3,2:T(1,128)S(1)}, u32[]{:S(2)}, u32[]{:S(2)}) async-start(f32[1,14,64,3]{1,0,3,2:T(1,128)} %bitcast.78), calls=%async_computation | async-start | bytes 196608 | tf_op jit(solution)/shard_map/all_to_all | solution.py:155
  132.1 10.7 %all-to-all-done = f32[1,14,64,3]{1,0,3,2:T(1,128)S(1)} async-done(((f32[1,14,64,3]{1,0,3,2:T(1,128)}), f32[1,14,64,3]{1,0,3,2:T(1,128)S(1)}, u32[]{:S(2)}, u32[]{:S(2)}) %all-to-all-start) | async-done | bytes 10784 | tf_op jit(solution)/shard_map/all_to_all | solution.py:155
  146.4 2.2 gather_fusion.5
  148.6 4.4 all-to-all-start.2
  153.7 10.0 %all-to-all-done.2 = f32[1,14,64,3]{1,0,3,2:T(1,128)S(1)} async-done(((f32[1,14,64,3]{1,0,3,2:T(1,128)}), f32[1,14,64,3]{1,0,3,2:T(1,128)S(1)}, u32[]{:S(2)}, u32[]{:S(2)}) %all-to-all-start.2) | async-done | bytes 10784 | tf_op jit(solution)/shard_map/all_to_all | solution.py:179
  169.3 2.5 copy.85
  171.8 1.9 convert_reduce_fusion.2
  173.7 6.8 %convert_reduce_fusion = (f32[128]{0:T(128)S(1)}, bf16[96,128,128]{2,1,0:T(8,128)(2,1)S(1)}) fusion(f32[96,128,128]{2,1,0:T(8,128)} %get-tuple-element.67, f32[128]{0:T(128)S(1)} %copy-done.9, bf16[14,96,128]{2,0,1:T(8,128)(2,1)S(1)} %get-tuple-element.58, bf16[128,14]{0,1:T(8,128)(2,1)S(1)} %copy-done.6), kind=kOutput, calls=%fused_computation.32 | convolution fusion | flops 78643072 | bytes 9785856 | tf_op jit(solution)/shard_map/mprc,hp->mrch/dot_general | solution.py:39
  180.6 4.7 %convert_reduce_fusion.1 = (f32[128]{0:T(128)S(1)}, bf16[96,128,128]{2,1,0:T(8,128)(2,1)S(1)}) fusion(f32[96,128,128]{2,1,0:T(8,128)S(1)} %bitcast.72, f32[128]{0:T(128)S(1)} %copy-done.10, bf16[96,128,128]{2,1,0:T(8,128)(2,1)S(1)} %get-tuple-element.73, bf16[128,128]{1,0:T(8,128)(2,1)S(1)} %copy-done.8), kind=kOutput, calls=%fused_computation.33 | convolution fusion | flops 437256064 | bytes 12616704 | tf_op jit(solution)/shard_map/mrcg,hg->mrch/dot_general | solution.py:39
  185.4 3.2 convolution_bitcast_fusion
  188.6 2.6 fusion
  192.8 74.2 %all-reduce.1 = (f32[128]{0:T(128)}, f32[128]{0:T(128)}, f32[128,14]{0,1:T(8,128)}, f32[14]{0:T(128)}, f32[]{:T(128)}) all-reduce(f32[128]{0:T(128)S(1)} %get-tuple-element.70, f32[128]{0:T(128)S(1)} %get-tuple-element.72, f32[128,14]{0,1:T(8,128)S(1)} %convolution_bitcast_fusion.1, ...), channel_id=1, replica_groups=mesh['dp'=4,'space'=64] {'dp','space'}, use_global_device_ids=true, to_apply=%region_9.10 | all-reduce | flops 2063 | bytes 16504 | tf_op jit(solution)/shard_map/psum | solution.py:189
  267.6 165.0 %all-reduce.5.cloned.1.call-done = (f32[3,3,32,128]{3,2,1,0:T(8,128)}, f32[128,128]{1,0:T(8,128)}) async-done(((f32[3,3,32,128]{3,2,1,0:T(8,128)}, f32[128,128]{1,0:T(8,128)}), (f32[3,3,32,128]{3,2,1,0:T(8,128)}, f32[128,128]{1,0:T(8,128)})) %all-reduce.5.cloned.1.call-update) | async-done | bytes 213008 | tf_op jit(solution)/shard_map/psum | solution.py:189
  (94 shorter events, 36.1 us)
Async XLA Ops:
  7.2 88.9 %copy-start = (bf16[3,3,32,128]{3,2,1,0:T(8,128)(2,1)S(1)}, bf16[3,3,32,128]{3,2,1,0:T(8,128)(2,1)}, u32[]{:S(2)}) copy-start(bf16[3,3,32,128]{3,2,1,0:T(8,128)(2,1)} %param.16) | copy-start | bytes 221188
  7.2 76.7 %copy-start.5 = (f32[1,14,192]{2,0,1:T(1,128)S(1)}, f32[1,14,192]{2,0,1:T(1,128)}, u32[]{:S(2)}) copy-start(f32[1,14,192]{2,0,1:T(1,128)} %param.15) | copy-start | bytes 32260
  8.7 84.1 %collective-permute-start = (bf16[1,32,1,128]{3,1,2,0:T(8,128)(2,1)S(1)}, bf16[1,32,1,128]{3,1,2,0:T(8,128)(2,1)S(1)}, u32[]{:S(2)}, u32[]{:S(2)}) collective-permute-start(bf16[1,32,1,128]{3,1,2,0:T(8,128)(2,1)S(1)} %get-tuple-element.61), channel_id=1, source_target_pairs={{0,1},{1,2},{2,3},{3,4},{4,5},{5,6},{6,7},{7,8},{8,9},{9,10},{10,1... | collective-permute-start | bytes 24584 | tf_op jit(solution)/shard_map/ppermute | solution.py:20
  13.3 79.5 %collective-permute-start.1 = (bf16[1,32,1,128]{3,1,2,0:T(8,128)(2,1)S(1)}, bf16[1,32,1,128]{3,1,2,0:T(8,128)(2,1)S(1)}, u32[]{:S(2)}, u32[]{:S(2)}) collective-permute-start(bf16[1,32,1,128]{3,1,2,0:T(8,128)(2,1)S(1)} %get-tuple-element.62), channel_id=1, source_target_pairs={{1,0},{2,1},{3,2},{4,3},{5,4},{6,5},{7,6},{8,7},{9,8},{10,9},{11,1... | collective-permute-start | bytes 24584 | tf_op jit(solution)/shard_map/ppermute | solution.py:23
  66.8 27.8 %copy-start.3 = (bf16[1,32,96,128]{3,2,1,0:T(8,128)(2,1)S(1)}, bf16[1,32,96,128]{3,2,1,0:T(8,128)(2,1)}, u32[]{:S(2)}) copy-start(bf16[1,32,96,128]{3,2,1,0:T(8,128)(2,1)} %param.11) | copy-start | bytes 2359300
  67.6 22.2 %all-to-all-start.1 = ((f32[1,1,64,3]{3,1,0,2:T(1,128)}), f32[1,1,64,3]{3,1,0,2:T(1,128)S(1)}, u32[]{:S(2)}, u32[]{:S(2)}) async-start(f32[1,1,64,3]{3,1,0,2:T(1,128)} %bitcast.12), calls=%async_computation.1 | async-start | bytes 65536 | tf_op jit(solution)/shard_map/all_to_all | solution.py:162
  96.1 2.9 copy-start.1
  99.0 2.8 copy-start.8
  99.0 2.8 copy-start.9
  99.0 2.8 copy-start.10
  101.8 6.2 %copy-start.2 = (f32[96,128,128]{2,1,0:T(8,128)}, f32[96,128,128]{2,1,0:T(8,128)S(1)}, u32[]{:S(2)}) copy-start(f32[96,128,128]{2,1,0:T(8,128)S(1)} %fusion.2) | copy-start | bytes 18874372
  101.8 6.2 %copy-start.6 = (bf16[128,14]{0,1:T(8,128)(2,1)S(1)}, bf16[128,14]{0,1:T(8,128)(2,1)}, u32[]{:S(2)}) copy-start(bf16[128,14]{0,1:T(8,128)(2,1)} %param.20) | copy-start | bytes 10756
  101.8 6.2 %copy-start.7 = (f32[14]{0:T(128)S(1)}, f32[14]{0:T(128)}, u32[]{:S(2)}) copy-start(f32[14]{0:T(128)} %param.21) | copy-start | bytes 172
  127.3 15.5 %all-to-all-start = ((f32[1,14,64,3]{1,0,3,2:T(1,128)}), f32[1,14,64,3]{1,0,3,2:T(1,128)S(1)}, u32[]{:S(2)}, u32[]{:S(2)}) async-start(f32[1,14,64,3]{1,0,3,2:T(1,128)} %bitcast.78), calls=%async_computation | async-start | bytes 196608 | tf_op jit(solution)/shard_map/all_to_all | solution.py:155
  148.6 15.1 %all-to-all-start.2 = ((f32[1,14,64,3]{1,0,3,2:T(1,128)}), f32[1,14,64,3]{1,0,3,2:T(1,128)S(1)}, u32[]{:S(2)}, u32[]{:S(2)}) async-start(f32[1,14,64,3]{1,0,3,2:T(1,128)} %bitcast.77), calls=%async_computation.2 | async-start | bytes 196608 | tf_op jit(solution)/shard_map/all_to_all | solution.py:179
  153.0 279.6 %all-reduce.5.cloned.1.call-start = ((), (), s32[]{:S(2)}) async-start(), calls=%async_computation.3 | async-start | bytes 425984 | tf_op jit(solution)/shard_map/psum | solution.py:189
  171.8 8.8 %slice-start.2 = ((s8[6291456]{0:T(1024)(128)(4,1)}), s8[4194304]{0:T(1024)(128)(4,1)S(1)}, s32[]{:S(2)}) async-start(s8[6291456]{0:T(1024)(128)(4,1)} %bitcast.71), calls=%async_computation.6 | async-start | bytes 8388608
  173.7 6.9 %copy-start.4 = (bf16[14,96,128]{2,0,1:T(8,128)(2,1)}, bf16[14,96,128]{2,0,1:T(8,128)(2,1)S(1)}, u32[]{:S(2)}) copy-start(bf16[14,96,128]{2,0,1:T(8,128)(2,1)S(1)} %get-tuple-element.58) | copy-start | bytes 1032196
  173.7 6.9 %slice-start.3 = ((s8[6291456]{0:T(1024)(128)(4,1)}), s8[2097152]{0:T(1024)(128)(4,1)S(1)}, s32[]{:S(2)}) async-start(s8[6291456]{0:T(1024)(128)(4,1)} %bitcast.71), calls=%async_computation.7 | async-start | bytes 4194304
  173.7 14.8 %slice-start = ((s8[7077888]{0:T(1024)(128)(4,1)}), s8[4194304]{0:T(1024)(128)(4,1)S(1)}, s32[]{:S(2)}) async-start(s8[7077888]{0:T(1024)(128)(4,1)} %bitcast.69), calls=%async_computation.4 | async-start | bytes 8388608
  180.6 7.9 %slice-start.1 = ((s8[7077888]{0:T(1024)(128)(4,1)}), s8[2883584]{0:T(1024)(128)(4,1)S(1)}, s32[]{:S(2)}) async-start(s8[7077888]{0:T(1024)(128)(4,1)} %bitcast.69), calls=%async_computation.5 | async-start | bytes 5767168
Sparse Core Ops, SparseCore 0:
  191.4 241.2 all-reduce.4
where the time goes:
time: 445 us; the launch traced here: 444 us
  waiting for transfers between devices  191 us (43%)
  local copies, waits for them, and re-layouts  88.8 us (20%)
  blocking collectives  74.2 us (17%)
  matrix products  29.7 us (7%)
  starting transfers between devices  28.6 us (6%)
  between operations  16.3 us (4%)
  other arithmetic  14.7 us (3%)
    psum x1, waiting for transfers between devices, on_device(): lax.psum((grads[0], grads[1], grads[2], grads[3], grads[4], grads[5], squ...  165 us
    psum x1, blocking collectives, on_device(): lax.psum((grads[0], grads[1], grads[2], grads[3], grads[4], grads[5], squ...  74.2 us
    scatter x1, local copies, waits for them, and re-layouts, route_tables(): jnp.zeros((count_all,), jnp.int32).at[owner_map]  45.4 us
    dot_general x8, matrix products, product(): return jnp.einsum(form, left, right, preferred_element_type=jnp.float32)  29.7 us
    all_to_all x1, starting transfers between devices, on_device(): lax.all_to_all(strip_weights[slot_block].reshape(1, 1, peers, capacity),...  12.9 us
    all_to_all x1, waiting for transfers between devices, on_device(): lax.all_to_all(strip_values[:, :, slot_block].reshape(members, pools, pee...  10.7 us
    unnamed x41, local copies, waits for them, and re-layouts  10 us
    all_to_all x1, waiting for transfers between devices, on_device(): lax.all_to_all(d_coarse[:, :, back_order].reshape(members, pools, peers,...  9.98 us
  transfers between devices with their start and end apart: 6, of which 4 were waited for; matrix products, arithmetic and copies ran while one was open for 14% of the time, Pallas kernels for 0%

commit v1 on v0

v1 whole, which is shorter than its diff:
```python
import functools
import math

import jax
import jax.numpy as jnp
from jax import lax
from jax.experimental import pallas as pl
from jax.experimental.pallas import tpu as pltpu
from jax.sharding import PartitionSpec as P

SIDE = 8


CUBIC = 0.044715
ROOT_TWO_PI = math.sqrt(2.0 / math.pi)


def halo_rows(block):
    count = lax.axis_size("space")
    forward = [(i, i + 1) for i in range(count - 1)]
    backward = [(target, source) for source, target in forward]
    above = lax.ppermute(block[-1:], "space", forward)
    below = lax.ppermute(block[:1], "space", backward)
    return above, below


def gelu_pair(pre):
    inner = ROOT_TWO_PI * (pre + CUBIC * pre * pre * pre)
    tanh_value = jnp.tanh(inner)
    value = 0.5 * pre * (1.0 + tanh_value)
    slope = 0.5 * (1.0 + tanh_value) + 0.5 * pre * (1.0 - tanh_value * tanh_value) * ROOT_TWO_PI * (
        1.0 + 3.0 * CUBIC * pre * pre
    )
    return (value, slope)


MESH = pl.DeviceIdType.MESH
EXACT = lax.Precision.HIGHEST
TURNS = 16
LINES = 32
PART = 2
SLOTS = 3
LANES = 16


def pack(values, picks):
    peers = picks[0].shape[0]
    rows = [
        lax.dot_general(values, pick, (((1,), (1,)), ((), ())), precision=EXACT, preferred_element_type=jnp.float32)
        for pick in picks
    ]
    rows.append(jnp.zeros((128 - LANES * len(picks), peers), jnp.float32))
    return jnp.concatenate(rows, axis=0).T


def unpack(block, picks):
    turned = block.T
    total = None
    for slot, pick in enumerate(picks):
        term = jnp.dot(
            turned[LANES * slot : LANES * (slot + 1)], pick, precision=EXACT, preferred_element_type=jnp.float32
        )
        total = term if total is None else total + term
    return total


def owner_picks(owners, me, blocks):
    peers = owners.shape[0]
    local = owners - me * blocks
    match = ((local >= 0) & (local < blocks)).astype(jnp.float32)
    row = lax.broadcasted_iota(jnp.int32, (blocks, blocks), 0)
    col = lax.broadcasted_iota(jnp.int32, (blocks, blocks), 1)
    before = (row < col).astype(jnp.float32)
    earlier = jnp.dot(match.astype(jnp.bfloat16), before.astype(jnp.bfloat16), preferred_element_type=jnp.float32)
    place = lax.broadcasted_iota(jnp.int32, (peers, blocks), 1).astype(jnp.float32)
    picks = []
    for slot in range(SLOTS):
        mine = match * (earlier == float(slot)).astype(jnp.float32)
        spot = jnp.sum(mine * local.astype(jnp.float32), axis=1, keepdims=True)
        picks.append((place == spot).astype(jnp.float32))
    return picks


def strip_picks(owned, peers, blocks):
    scaled = (owned.astype(jnp.float32) + 0.5) * (1.0 / blocks)
    target = jnp.floor(scaled)
    row = lax.broadcasted_iota(jnp.int32, (blocks, blocks), 0)
    col = lax.broadcasted_iota(jnp.int32, (blocks, blocks), 1)
    spread = jnp.broadcast_to(target, (blocks, blocks))
    column = jnp.sum(jnp.where(row == col, spread, 0.0), axis=1, keepdims=True)
    same = jnp.where((column == spread) & (row < col), 1.0, 0.0)
    rank = jnp.sum(same, axis=0, keepdims=True)
    peer = lax.broadcasted_iota(jnp.int32, (peers, blocks), 0).astype(jnp.float32)
    return [
        ((peer == target) & (rank == float(slot))).astype(jnp.float32) for slot in range(SLOTS)
    ]


def row_copy(peers, me, step, send_ref, recv_ref, send_sems, recv_sems):
    peer = lax.rem(me + step, peers)
    return pltpu.make_async_remote_copy(
        src_ref=send_ref.at[peer],
        dst_ref=recv_ref.at[me],
        send_sem=send_sems.at[step],
        recv_sem=recv_sems.at[step],
        device_id=(lax.axis_index("dp"), peer),
        device_id_type=MESH,
    )


def targets_kernel(
    peers, blocks, owners_ref, targets_ref, strip_ref, owner_ref, here_ref,
    send, recv, held, send_sems, recv_sems
):
    me = lax.axis_index("space")
    dp = lax.axis_index("dp")
    barrier = pltpu.get_barrier_semaphore()

    def greet(step, carry):
        pl.semaphore_signal(
            barrier, inc=1, device_id=(dp, lax.rem(me + step, peers)), device_id_type=MESH
        )
        return carry

    lax.fori_loop(1, peers, greet, 0)
    picks = owner_picks(owners_ref[...], me, blocks)
    for slot in range(SLOTS):
        owner_ref[slot] = picks[slot]
    pools = targets_ref.shape[0]
    held[...] = jnp.zeros_like(held)
    held[0:pools, :] = targets_ref[...]
    send[:, 0, :] = pack(held[...], picks)
    strip = strip_picks(owners_ref[pl.ds(me, 1), :], peers, blocks)
    for slot in range(SLOTS):
        strip_ref[slot] = strip[slot]
    pl.semaphore_wait(barrier, peers - 1)

    def begin(step, carry):
        row_copy(peers, me, step, send, recv, send_sems, recv_sems).start()
        return carry

    def finish(step, carry):
        row_copy(peers, me, step, send, recv, send_sems, recv_sems).wait()
        return carry

    lax.fori_loop(1, peers, begin, 0)
    recv[pl.ds(me, 1)] = send[pl.ds(me, 1)]
    lax.fori_loop(1, peers, finish, 0)
    here_ref[...] = unpack(recv[:, 0, :], strip)


def reduce_kernel(
    peers, ways, grads_ref, pred_ref, strip_ref, owner_ref, out_ref, coarse_ref,
    send, recv, got, part, got_part, whole, send_sems, recv_sems, out_sems, in_sems, own_sem
):
    me = lax.axis_index("space")
    x = lax.axis_index("dp")
    span = ways * 2
    z = me // span
    y = lax.rem(me, span) // 2
    core = lax.rem(me, 2)
    flat = x * ways + y
    deep = z * 2 + core

    def plane(step):
        other = lax.rem(flat + step, TURNS)
        return other, (other // ways, z * span + lax.rem(other, ways) * 2 + core)

    def line(step):
        other = lax.rem(deep + step, TURNS)
        return other, (x, (other // 2) * span + y * 2 + lax.rem(other, 2))

    barrier = pltpu.get_barrier_semaphore()

    def greet(step, carry):
        pl.semaphore_signal(barrier, inc=1, device_id=(x, lax.rem(me + step, peers)), device_id_type=MESH)
        return carry

    def greet_plane(step, carry):
        pl.semaphore_signal(barrier, inc=1, device_id=plane(step)[1], device_id_type=MESH)
        return carry

    lax.fori_loop(1, peers, greet, 0)
    lax.fori_loop(1, TURNS, greet_plane, 0)
    send[:, 0, :] = pack(pred_ref[...], [strip_ref[slot] for slot in range(SLOTS)])
    pl.semaphore_wait(barrier, peers - 1 + TURNS - 1)

    def remote(src, dst, phase, step, device):
        return pltpu.make_async_remote_copy(
            src_ref=src,
            dst_ref=dst,
            send_sem=out_sems.at[phase, step],
            recv_sem=in_sems.at[phase, step],
            device_id=device,
            device_id_type=MESH,
        )

    def scatter_plane(step):
        other, device = plane(step)
        return remote(grads_ref.at[other], got.at[step - 1], 0, step, device)

    def scatter_line(step):
        other, device = line(step)
        return remote(part.at[other], got_part.at[step - 1], 1, step, device)

    def gather_line(step):
        return remote(whole.at[deep], whole.at[deep], 2, step, line(step)[1])

    def gather_plane(step):
        return remote(out_ref.at[flat], out_ref.at[flat], 3, step, plane(step)[1])

    def start_all(build):
        def body(step, carry):
            build(step).start()
            return carry

        lax.fori_loop(1, TURNS, body, 0)

    def wait_all(build):
        def body(step, carry):
            build(step).wait()
            return carry

        lax.fori_loop(1, TURNS, body, 0)

    start_all(scatter_plane)

    def begin(step, carry):
        row_copy(peers, me, step, send, recv, send_sems, recv_sems).start()
        return carry

    def finish(step, carry):
        row_copy(peers, me, step, send, recv, send_sems, recv_sems).wait()
        return carry

    lax.fori_loop(1, peers, begin, 0)
    recv[pl.ds(me, 1)] = send[pl.ds(me, 1)]

    wait_all(scatter_plane)
    total = grads_ref[flat]
    for step in range(TURNS - 1):
        total = total + got[step]
    for turn in range(TURNS):
        part[turn] = total[PART * turn : PART * (turn + 1)]
    start_all(scatter_line)
    wait_all(scatter_line)
    piece = part[deep]
    for step in range(TURNS - 1):
        piece = piece + got_part[step]
    whole[deep] = piece
    start_all(gather_line)
    wait_all(gather_line)
    own = pltpu.make_async_copy(whole, out_ref.at[flat], own_sem)
    own.start()
    own.wait()
    start_all(gather_plane)
    lax.fori_loop(1, peers, finish, 0)
    coarse_ref[...] = unpack(recv[:, 0, :], [owner_ref[slot] for slot in range(SLOTS)])
    wait_all(gather_plane)


def vmem(count):
    return [pl.BlockSpec(memory_space=pltpu.VMEM)] * count


def route_targets(owner_map, targets, peers, blocks):
    picks = jax.ShapeDtypeStruct((SLOTS, peers, blocks), jnp.float32)
    return pl.pallas_call(
        functools.partial(targets_kernel, peers, blocks),
        out_shape=(picks, picks, jax.ShapeDtypeStruct((LANES, blocks), jnp.float32)),
        in_specs=vmem(2),
        out_specs=tuple(vmem(3)),
        scratch_shapes=[
            pltpu.VMEM((peers, 1, 128), jnp.float32),
            pltpu.VMEM((peers, 1, 128), jnp.float32),
            pltpu.VMEM((LANES, blocks), jnp.float32),
            pltpu.SemaphoreType.DMA((peers,)),
            pltpu.SemaphoreType.DMA((peers,)),
        ],
        compiler_params=pltpu.CompilerParams(collective_id=0, has_side_effects=True),
        name="route_targets",
    )(owner_map.reshape(peers, blocks), targets)


def reduce_all(grads, pred, strip, owner, peers, blocks):
    ways = lax.axis_size("dp")
    return pl.pallas_call(
        functools.partial(reduce_kernel, peers, ways),
        out_shape=(
            jax.ShapeDtypeStruct((TURNS, TURNS, PART, 128), jnp.float32),
            jax.ShapeDtypeStruct((LANES, blocks), jnp.float32),
        ),
        in_specs=vmem(4),
        out_specs=tuple(vmem(2)),
        scratch_shapes=[
            pltpu.VMEM((peers, 1, 128), jnp.float32),
            pltpu.VMEM((peers, 1, 128), jnp.float32),
            pltpu.VMEM((TURNS - 1, LINES, 128), jnp.float32),
            pltpu.VMEM((TURNS, PART, 128), jnp.float32),
            pltpu.VMEM((TURNS - 1, PART, 128), jnp.float32),
            pltpu.VMEM((TURNS, PART, 128), jnp.float32),
            pltpu.SemaphoreType.DMA((peers,)),
            pltpu.SemaphoreType.DMA((peers,)),
            pltpu.SemaphoreType.DMA((4, TURNS)),
            pltpu.SemaphoreType.DMA((4, TURNS)),
            pltpu.SemaphoreType.DMA,
        ],
        compiler_params=pltpu.CompilerParams(collective_id=1, has_side_effects=True),
        name="reduce_all",
    )(grads, pred, strip, owner)


NT = (((1,), (1,)), ((), ()))
ONES = 16


def dot(left, right, dims=(((1,), (0,)), ((), ()))):
    return lax.dot_general(left, right, dims, preferred_element_type=jnp.float32)


def exact_dot(left, right, dims=(((1,), (0,)), ((), ()))):
    return lax.dot_general(left, right, dims, precision=EXACT, preferred_element_type=jnp.float32)


def column_of(row):
    width = row.shape[1]
    return jnp.broadcast_to(row, (width, width)).T[:, 0:1]


def shift_rows(block):
    wide = block.astype(jnp.float32)
    columns = wide.shape[2]
    place = lax.broadcasted_iota(jnp.int32, wide.shape, 2)
    left = jnp.where(place == 0, 0.0, pltpu.roll(wide, 1, 2))
    right = jnp.where(place == columns - 1, 0.0, pltpu.roll(wide, columns - 1, 2))
    return jnp.concatenate([left.astype(jnp.bfloat16), block, right.astype(jnp.bfloat16)], axis=1)


def network_kernel(
    count_all, pools, x_ref, above_ref, below_ref, frac_ref, mask_ref, here_ref,
    conv_ref, conv_bias_ref, mix_ref, mix_bias_ref, out_ref, out_bias_ref,
    flat_ref, pred_ref,
    shifted, stacked, row_buf, conv_acc, mix_acc, out_acc, bias_acc, square_acc
):
    rows, channels, columns = x_ref.shape
    taps, width = conv_ref.shape
    cells = SIDE * columns
    blocks = here_ref.shape[1]
    across = columns // SIDE

    shifted[0:1] = shift_rows(above_ref[...])
    shifted[rows + 1 : rows + 2] = shift_rows(below_ref[...])

    def shift_some(step, carry):
        shifted[pl.ds(step * SIDE + 1, SIDE)] = shift_rows(x_ref[pl.ds(step * SIDE, SIDE)])
        return carry

    lax.fori_loop(0, rows // SIDE, shift_some, 0)
    stacked[taps : taps + ONES, :] = jnp.ones((ONES, cells), jnp.bfloat16)

    conv_t = conv_ref[...].astype(jnp.float32).T.astype(jnp.bfloat16)
    mix = mix_ref[...]
    mix_t = mix.astype(jnp.float32).T.astype(jnp.bfloat16)
    row_buf[...] = jnp.zeros_like(row_buf)
    row_buf[0:pools, :] = out_ref[...].astype(jnp.float32)
    out_wide = row_buf[...]
    out_t = out_wide[0:LANES].astype(jnp.bfloat16)
    out_w = out_wide.T[:, 0:LANES].astype(jnp.bfloat16)
    row_buf[...] = jnp.zeros_like(row_buf)
    row_buf[0:1, 0:pools] = out_bias_ref[...]
    conv_bias = column_of(conv_bias_ref[...])
    mix_bias = column_of(mix_bias_ref[...])
    out_bias = column_of(row_buf[0:1, :])[0:LANES]

    conv_acc[...] = jnp.zeros_like(conv_acc)
    mix_acc[...] = jnp.zeros_like(mix_acc)
    out_acc[...] = jnp.zeros_like(out_acc)
    bias_acc[...] = jnp.zeros_like(bias_acc)
    square_acc[...] = jnp.zeros_like(square_acc)
    pred_ref[...] = jnp.zeros_like(pred_ref)
    here = here_ref[...]
    scale = math.sqrt(count_all)

    def tile(step, carry):
        base = step * SIDE
        for line in range(SIDE):
            window = shifted[pl.ds(base + line, 3)]
            stacked[0:taps, line * columns : (line + 1) * columns] = window.reshape(taps, columns)
        patch = stacked[0:taps, :]
        pre_one = dot(conv_t, patch) + conv_bias
        value_one, slope_one = gelu_pair(pre_one)
        hidden_one = value_one.astype(jnp.bfloat16)
        pre_two = dot(mix_t, hidden_one) + mix_bias
        value_two, slope_two = gelu_pair(pre_two)
        hidden_two = value_two.astype(jnp.bfloat16)
        raw = dot(out_t, hidden_two) + out_bias
        window = pl.ds(pl.multiple_of(base, SIDE), SIDE)
        weight = frac_ref[window, :] * mask_ref[window, :].astype(jnp.float32)
        weight_row = jnp.concatenate([weight[line : line + 1] for line in range(SIDE)], axis=1)
        decay = jnp.exp(-jnp.abs(raw))
        density = (jnp.maximum(raw, 0.0) + jnp.log1p(decay)) * weight_row
        folded = density[:, 0:columns]
        for line in range(1, SIDE):
            folded = folded + density[:, line * columns : (line + 1) * columns]
        column = lax.broadcasted_iota(jnp.int32, (columns, blocks), 0)
        block = lax.broadcasted_iota(jnp.int32, (columns, blocks), 1)
        first = block - step * across
        member = ((column >= first * SIDE) & (column < first * SIDE + SIDE)).astype(jnp.float32)
        sums = exact_dot(folded, member)
        weight_sum = exact_dot(
            jnp.broadcast_to(jnp.sum(weight, axis=0, keepdims=True), (SIDE, columns)), member
        )[0:1]
        denom = jnp.maximum(weight_sum, 1.0)
        pred = sums / denom
        pred_ref[...] += pred
        pool = lax.broadcasted_iota(jnp.int32, pred.shape, 0)
        lane = lax.broadcasted_iota(jnp.int32, pred.shape, 1)
        inside = (pool < pools) & (lane >= step * across) & (lane < step * across + across)
        residual = jnp.where(inside, pred - here, 0.0)
        square_acc[...] += residual * residual
        d_block = residual / (scale * denom)
        d_columns = exact_dot(d_block, member, NT)
        d_cells = jnp.concatenate([d_columns] * SIDE, axis=1)
        d_raw = (d_cells * weight_row * jax.nn.sigmoid(raw)).astype(jnp.bfloat16)
        d_wide = d_raw.astype(jnp.float32)
        bias_sum = d_wide[:, 0:columns]
        for line in range(1, SIDE):
            bias_sum = bias_sum + d_wide[:, line * columns : (line + 1) * columns]
        bias_acc[...] += bias_sum
        out_acc[...] += dot(d_raw, hidden_two, NT)
        d_two = (dot(out_w, d_raw) * slope_two).astype(jnp.bfloat16)
        ones = jnp.ones((ONES, cells), jnp.bfloat16)
        mix_acc[...] += dot(jnp.concatenate([hidden_one, ones], axis=0), d_two, NT)
        d_one = (dot(mix, d_two) * slope_one).astype(jnp.bfloat16)
        conv_acc[...] += dot(stacked[...], d_one, NT)
        return carry

    lax.fori_loop(0, rows // SIDE, tile, 0)
    row_buf[...] = jnp.zeros_like(row_buf)
    row_buf[0:LANES, :] = bias_acc[...]
    out_bias_row = exact_dot(jnp.ones((SIDE, columns), jnp.float32), row_buf[...], NT)[0:1]
    squares = jnp.sum(jnp.sum(square_acc[...], axis=1, keepdims=True), axis=0, keepdims=True)
    conv_all = conv_acc[...]
    mix_all = mix_acc[...]
    flat_ref[0:taps, :] = conv_all[0:taps]
    flat_ref[taps : taps + width, :] = mix_all[0:width]
    base = taps + width
    flat_ref[base : base + LANES, :] = out_acc[...]
    base += LANES
    flat_ref[base:, :] = jnp.zeros((flat_ref.shape[0] - base, width), jnp.float32)
    flat_ref[base : base + 1, :] = conv_all[taps : taps + 1]
    flat_ref[base + 1 : base + 2, :] = mix_all[width : width + 1]
    flat_ref[base + 2 : base + 3, :] = out_bias_row
    flat_ref[base + 3 : base + 4, :] = jnp.broadcast_to(squares, (1, width))


def run_network(count_all, pools, x, above, below, frac, mask, here, conv, conv_bias, mix, mix_bias, out, out_bias):
    rows, channels, columns = x.shape
    taps, width = conv.shape
    blocks = here.shape[1]
    return pl.pallas_call(
        functools.partial(network_kernel, count_all, pools),
        out_shape=(
            jax.ShapeDtypeStruct((TURNS * LINES, width), jnp.float32),
            jax.ShapeDtypeStruct((LANES, blocks), jnp.float32),
        ),
        in_specs=vmem(12),
        out_specs=tuple(vmem(2)),
        scratch_shapes=[
            pltpu.VMEM((rows + 2, 3 * channels, columns), jnp.bfloat16),
            pltpu.VMEM((taps + ONES, SIDE * columns), jnp.bfloat16),
            pltpu.VMEM((width, columns), jnp.float32),
            pltpu.VMEM((taps + ONES, width), jnp.float32),
            pltpu.VMEM((width + ONES, width), jnp.float32),
            pltpu.VMEM((LANES, width), jnp.float32),
            pltpu.VMEM((LANES, columns), jnp.float32),
            pltpu.VMEM((LANES, blocks), jnp.float32),
        ],
        name="network",
    )(x, above, below, frac, mask, here, conv, conv_bias, mix, mix_bias, out, out_bias)


def finish_kernel(
    count_all, pools, sum_ref, coarse_ref,
    pred_out, conv_out, conv_bias_out, mix_out, mix_bias_out, out_out, out_bias_out, loss_out
):
    taps = conv_out.shape[0]
    width = mix_out.shape[0]
    for turn in range(TURNS):
        lines = sum_ref[turn].reshape(LINES, width)
        first = turn * LINES
        if first < taps:
            conv_out[first : first + LINES, :] = lines
        elif first < taps + width:
            mix_out[first - taps : first - taps + LINES, :] = lines
        elif first == taps + width:
            out_out[...] = lines[0:pools]
            conv_bias_out[...] = lines[LANES : LANES + 1]
            mix_bias_out[...] = lines[LANES + 1 : LANES + 2]
            out_bias_out[...] = lines[LANES + 2 : LANES + 3, 0:pools]
            loss_out[...] = 0.5 * lines[LANES + 3 : LANES + 4, 0:1] / count_all
    pred_out[...] = coarse_ref[0:pools, :]


def finish(count_all, pools, taps, summed, coarse):
    width = summed.shape[-1]
    shapes = [
        (pools, coarse.shape[1]), (taps, width), (1, width), (width, width), (1, width), (pools, width),
        (1, pools), (1, 1),
    ]
    return pl.pallas_call(
        functools.partial(finish_kernel, count_all, pools),
        out_shape=tuple(jax.ShapeDtypeStruct(shape, jnp.float32) for shape in shapes),
        in_specs=vmem(2),
        out_specs=tuple(vmem(len(shapes))),
        name="finish",
    )(summed, coarse)


def on_device(
    fields,
    land_mask,
    land_frac,
    owner_map,
    targets,
    conv_weight,
    conv_bias,
    mix_weight,
    mix_bias,
    out_weight,
    out_bias,
):
    peers = lax.axis_size("space")
    pools = out_weight.shape[1]
    width = conv_bias.shape[0]
    blocks = fields.shape[2] // SIDE * (fields.shape[3] // SIDE)
    count_all = lax.axis_size("dp") * pools * owner_map.shape[0]
    x = fields[0].transpose(1, 0, 2)
    above, below = halo_rows(x)
    strip, owner, here = route_targets(owner_map, targets[0], peers, blocks)
    conv = conv_weight.reshape(-1, width)
    flat, pred = run_network(
        count_all, pools, x, above, below, land_frac, land_mask, here, conv, conv_bias[None],
        mix_weight, mix_bias[None], out_weight.T, out_bias[None],
    )
    summed, coarse = reduce_all(
        flat.reshape(TURNS, LINES, width), pred, strip, owner, peers, blocks
    )
    pred_out, conv_out, conv_bias_out, mix_out, mix_bias_out, out_out, out_bias_out, loss = finish(
        count_all, pools, conv.shape[0], summed, coarse
    )
    return (
        pred_out[None],
        conv_out.reshape(conv_weight.shape),
        conv_bias_out[0],
        mix_out,
        mix_bias_out[0],
        out_out.T,
        out_bias_out[0],
        loss[0, 0],
    )


def solution(mesh):
    placed = (
        P("dp", None, "space", None),
        P("space", None),
        P("space", None),
        P(),
        P("dp", None, "space"),
        P(),
        P(),
        P(),
        P(),
        P(),
        P(),
    )
    return jax.shard_map(
        on_device,
        mesh=mesh,
        in_specs=placed,
        out_specs=(P("dp", None, "space"), P(), P(), P(), P(), P(), P(), P()),
        check_vma=False,
    )
```

time: 445 us -> 96.1 us (0.22)
  waiting for transfers between devices: 191 us -> 0.01 us
  local copies, waits for them, and re-layouts: 88.8 us -> 4.7 us
  Pallas kernels: 0 us -> 83.1 us
  blocking collectives: 74.2 us -> 0 us
  matrix products: 29.7 us -> 0 us
  starting transfers between devices: 28.6 us -> 7.2 us
  between operations: 16.3 us -> 0.75 us
  other arithmetic: 14.7 us -> 0 us
    psum x1 -> x0, waiting for transfers between devices: 165 us -> none  [on_device(): lax.psum((grads[0], grads[1], grads[2], grads[3], grads[4], grads[5], squ...]
    pallas_call x0 -> x4, Pallas kernels: none -> 83.1 us  [the longest x1 33.1 us: reduce_all(): pl.pallas_call(functools.partial(reduce_kernel, peers, ways), out_shape=(...]
    psum x1 -> x0, blocking collectives: 74.2 us -> none  [on_device(): lax.psum((grads[0], grads[1], grads[2], grads[3], grads[4], grads[5], squ...]
    scatter x3 -> x0, local copies, waits for them, and re-layouts: 48 us -> none  [the longest x1 45.4 us: route_tables(): jnp.zeros((count_all,), jnp.int32).at[owner_map]]
    dot_general x8 -> x0, matrix products: 29.7 us -> none  [product(): return jnp.einsum(form, left, right, preferred_element_type=jnp.float32)]
    all_to_all x3 -> x0, waiting for transfers between devices: 26.4 us -> none  [the longest x1 10.7 us: on_device(): lax.all_to_all(strip_values[:, :, slot_block].reshape(members, pools, pee...]
    all_to_all x3 -> x0, starting transfers between devices: 22 us -> none  [the longest x1 12.9 us: on_device(): lax.all_to_all(strip_weights[slot_block].reshape(1, 1, peers, capacity),...]
    reshape x7 -> x1, local copies, waits for them, and re-layouts: 11.9 us -> 0.71 us  [route_targets(): owner_map.reshape(peers, blocks)]
  transfers between devices with their start and end apart: 6 -> 2, of which waited for: 4 -> 0; matrix products, arithmetic and copies ran while one was open for 14% -> 1% of each run, Pallas kernels for 0% -> 19%
where the time goes in v1:
time: 96.1 us; the launch traced here: 95.8 us
  Pallas kernels  83.1 us (86%)
  starting transfers between devices  7.2 us (7%)
  local copies, waits for them, and re-layouts  4.7 us (5%)
    pallas_call x1, Pallas kernels, reduce_all(): pl.pallas_call(functools.partial(reduce_kernel, peers, ways), out_shape=(...  33.1 us
    pallas_call x1, Pallas kernels, run_network(): pl.pallas_call(functools.partial(network_kernel, count_all, pools), out_s...  30.2 us
    pallas_call x1, Pallas kernels, route_targets(): pl.pallas_call(functools.partial(targets_kernel, peers, blocks), out_shap...  18.1 us
    ppermute x1, starting transfers between devices, halo_rows(): below = lax.ppermute(block[:1], 'space', backward)  5.28 us
    unnamed x13, local copies, waits for them, and re-layouts  3.99 us
  transfers between devices with their start and end apart: 2, of which 0 were waited for; matrix products, arithmetic and copies ran while one was open for 1% of the time, Pallas kernels for 19%

profile of v1, /device:TPU:1, one launch (start us, length us, event | category | flops | bytes accessed | tf_op | source)
XLA Modules:
  0.0 95.8 jit_solution(17856043088416694635)
XLA Ops:
  0.6 0.0 copy-start.2
  0.6 1.4 %copy.24 = bf16[1,32,96,128]{3,1,2,0:T(8,128)(2,1)S(1)} copy(bf16[1,32,96,128]{3,2,1,0:T(8,128)(2,1)} %param.11) | data formatting | bytes 1572864 | tf_op args[0]
  2.1 0.0 copy-start
  2.1 0.0 copy-start.1
  2.1 5.3 %collective-permute-start.1 = (bf16[1,32,128]{2,1,0:T(8,128)(2,1)S(1)}, bf16[1,32,128]{2,1,0:T(8,128)(2,1)S(1)}, u32[]{:S(2)}, u32[]{:S(2)}) collective-permute-start(bf16[1,32,128]{2,1,0:T(8,128)(2,1)S(1)} %get-tuple-element.46), channel_id=1, source_target_pairs={{1,0},{2,1},{3,2},{4,3},{5,4},{6,5},{7,6},{8,7},{9,8},{10,9},{11,1... | collective-permute-start | bytes 24584 | tf_op jit(solution)/shard_map/ppermute | solution.py:23
  7.4 1.9 %collective-permute-start = (bf16[1,32,128]{2,1,0:T(8,128)(2,1)S(1)}, bf16[1,32,128]{2,1,0:T(8,128)(2,1)S(1)}, u32[]{:S(2)}, u32[]{:S(2)}) collective-permute-start(bf16[1,32,128]{2,1,0:T(8,128)(2,1)S(1)} %get-tuple-element.47), channel_id=1, source_target_pairs={{0,1},{1,2},{2,3},{3,4},{4,5},{5,6},{6,7},{7,8},{8,9},{9,10},{10,1... | collective-permute-start | bytes 24584 | tf_op jit(solution)/shard_map/ppermute | solution.py:22
  9.3 0.0 copy-done.2
  9.3 0.6 copy.25
  10.0 0.0 copy-done.1
  10.0 0.7 reshape.28.owners_ref
  10.7 18.1 %route_targets.1 = (f32[3,64,192]{2,1,0:T(8,128)}, f32[3,64,192]{2,1,0:T(8,128)}, f32[16,192]{1,0:T(8,128)}) custom-call(s32[64,192]{1,0:T(8,128)} %reshape.28.owners_ref, f32[14,192]{1,0:T(8,128)} %bitcast.25), custom_call_target="tpu_custom_call" | custom-call | tf_op jit(solution)/shard_map/route_targets/pallas_call | solution.py:268
  28.8 0.0 collective-permute-done.1.below_ref
  28.8 0.0 copy-start.3
  28.8 0.0 collective-permute-done.above_ref
  28.8 0.0 copy-start.4
  28.9 0.0 copy-done
  28.9 0.6 copy-done.3
  29.4 0.0 copy-done.4
  29.4 30.2 %network.1 = (f32[512,128]{1,0:T(8,128)}, f32[16,192]{1,0:T(8,128)}) custom-call(bf16[96,32,128]{2,1,0:T(8,128)(2,1)} %bitcast.22, bf16[1,32,128]{2,1,0:T(8,128)(2,1)} %copy-done.4, bf16[1,32,128]{2,1,0:T(8,128)(2,1)} %copy-done.3, f32[96,128]{1,0:T(8,128)} %frac_ref.1, s32[96,128]{1,0:T(8,128)} %mask_ref.1, f32[16,192]{1,0:T(8,128)} %get-tuple-element.23.here_ref, ...), custom_call_target="tpu_custom_call" | custom-call | tf_op jit(solution)/shard_map/network/pallas_call | solution.py:461
  59.7 33.1 %reduce_all.1 = (f32[16,16,2,128]{3,2,1,0:T(2,128)}, f32[16,192]{1,0:T(8,128)}) custom-call(f32[16,32,128]{2,1,0:T(8,128)} %bitcast.23, f32[16,192]{1,0:T(8,128)} %get-tuple-element.25.pred_ref, f32[3,64,192]{2,1,0:T(8,128)} %get-tuple-element.26.strip_ref, f32[3,64,192]{2,1,0:T(8,128)} %get-tuple-element.27.owner_ref), custom_call_target="tpu_custom_call" | custom-call | tf_op jit(solution)/shard_map/reduce_all/pallas_call | solution.py:287
  92.7 1.7 %finish.1 = (f32[14,192]{1,0:T(8,128)}, f32[288,128]{1,0:T(8,128)}, f32[1,128]{1,0:T(1,128)}, f32[128,128]{1,0:T(8,128)}, f32[1,128]{1,0:T(1,128)}, /*index=5*/f...) custom-call(f32[16,16,2,128]{3,2,1,0:T(2,128)} %get-tuple-element.28.sum_ref, f32[16,192]{1,0:T(8,128)} %get-tuple-element.29.coarse_ref), custom_call_target="tpu_custom_call" | custom-call | tf_op jit(solution)/shard_map/finish/pallas_call | solution.py:511
  94.4 1.3 %copy.20 = f32[1,14,192]{2,0,1:T(1,128)} copy(f32[1,14,192]{2,1,0:T(8,128)} %bitcast.26) | data formatting | bytes 21504
  (1 shorter events, 0.0 us)
Async XLA Ops:
  0.6 8.7 %copy-start.2 = (f32[1,14,192]{2,0,1:T(1,128)S(1)}, f32[1,14,192]{2,0,1:T(1,128)}, u32[]{:S(2)}) copy-start(f32[1,14,192]{2,0,1:T(1,128)} %param.15) | copy-start | bytes 32260
  2.1 26.8 %copy-start = (bf16[1,32,96,128]{3,1,2,0:T(8,128)(2,1)}, bf16[1,32,96,128]{3,1,2,0:T(8,128)(2,1)S(1)}, u32[]{:S(2)}) copy-start(bf16[1,32,96,128]{3,1,2,0:T(8,128)(2,1)S(1)} %copy.24) | copy-start | bytes 2359300
  2.1 7.9 %copy-start.1 = (s32[12288]{0:T(1024)S(1)}, s32[12288]{0:T(1024)}, u32[]{:S(2)}) copy-start(s32[12288]{0:T(1024)} %param.14) | copy-start | bytes 147460
  2.1 26.7 %collective-permute-start.1 = (bf16[1,32,128]{2,1,0:T(8,128)(2,1)S(1)}, bf16[1,32,128]{2,1,0:T(8,128)(2,1)S(1)}, u32[]{:S(2)}, u32[]{:S(2)}) collective-permute-start(bf16[1,32,128]{2,1,0:T(8,128)(2,1)S(1)} %get-tuple-element.46), channel_id=1, source_target_pairs={{1,0},{2,1},{3,2},{4,3},{5,4},{6,5},{7,6},{8,7},{9,8},{10,9},{11,1... | collective-permute-start | bytes 24584 | tf_op jit(solution)/shard_map/ppermute | solution.py:23
  7.4 21.4 %collective-permute-start = (bf16[1,32,128]{2,1,0:T(8,128)(2,1)S(1)}, bf16[1,32,128]{2,1,0:T(8,128)(2,1)S(1)}, u32[]{:S(2)}, u32[]{:S(2)}) collective-permute-start(bf16[1,32,128]{2,1,0:T(8,128)(2,1)S(1)} %get-tuple-element.47), channel_id=1, source_target_pairs={{0,1},{1,2},{2,3},{3,4},{4,5},{5,6},{6,7},{7,8},{8,9},{9,10},{10,1... | collective-permute-start | bytes 24584 | tf_op jit(solution)/shard_map/ppermute | solution.py:22
  28.8 0.6 copy-start.3
  28.8 0.6 copy-start.4

commit v2 on v1

v2 whole, which is shorter than its diff:
```python
import functools
import math

import jax
import jax.numpy as jnp
from jax import lax
from jax.experimental import pallas as pl
from jax.experimental.pallas import tpu as pltpu
from jax.sharding import PartitionSpec as P

SIDE = 8


CUBIC = 0.044715
ROOT_TWO_PI = math.sqrt(2.0 / math.pi)


def gelu_pair(pre):
    inner = ROOT_TWO_PI * (pre + CUBIC * pre * pre * pre)
    tanh_value = jnp.tanh(inner)
    value = 0.5 * pre * (1.0 + tanh_value)
    slope = 0.5 * (1.0 + tanh_value) + 0.5 * pre * (1.0 - tanh_value * tanh_value) * ROOT_TWO_PI * (
        1.0 + 3.0 * CUBIC * pre * pre
    )
    return (value, slope)


MESH = pl.DeviceIdType.MESH
EXACT = lax.Precision.HIGHEST
TURNS = 16
LINES = 32
PART = 2
SLOTS = 3
LANES = 16


def pack(values, picks):
    peers = picks[0].shape[0]
    rows = [
        lax.dot_general(values, pick, (((1,), (1,)), ((), ())), precision=EXACT, preferred_element_type=jnp.float32)
        for pick in picks
    ]
    rows.append(jnp.zeros((128 - LANES * len(picks), peers), jnp.float32))
    return jnp.concatenate(rows, axis=0).T


def unpack(block, picks):
    turned = block.T
    total = None
    for slot, pick in enumerate(picks):
        term = jnp.dot(
            turned[LANES * slot : LANES * (slot + 1)], pick, precision=EXACT, preferred_element_type=jnp.float32
        )
        total = term if total is None else total + term
    return total


def owner_picks(owners, me, blocks):
    peers = owners.shape[0]
    local = owners - me * blocks
    match = ((local >= 0) & (local < blocks)).astype(jnp.float32)
    row = lax.broadcasted_iota(jnp.int32, (blocks, blocks), 0)
    col = lax.broadcasted_iota(jnp.int32, (blocks, blocks), 1)
    before = (row < col).astype(jnp.float32)
    earlier = jnp.dot(match.astype(jnp.bfloat16), before.astype(jnp.bfloat16), preferred_element_type=jnp.float32)
    place = lax.broadcasted_iota(jnp.int32, (peers, blocks), 1).astype(jnp.float32)
    picks = []
    for slot in range(SLOTS):
        mine = match * (earlier == float(slot)).astype(jnp.float32)
        spot = jnp.sum(mine * local.astype(jnp.float32), axis=1, keepdims=True)
        picks.append((place == spot).astype(jnp.float32))
    return picks


def strip_picks(owned, peers, blocks):
    scaled = (owned.astype(jnp.float32) + 0.5) * (1.0 / blocks)
    target = jnp.floor(scaled)
    row = lax.broadcasted_iota(jnp.int32, (blocks, blocks), 0)
    col = lax.broadcasted_iota(jnp.int32, (blocks, blocks), 1)
    spread = jnp.broadcast_to(target, (blocks, blocks))
    column = jnp.sum(jnp.where(row == col, spread, 0.0), axis=1, keepdims=True)
    same = jnp.where((column == spread) & (row < col), 1.0, 0.0)
    rank = jnp.sum(same, axis=0, keepdims=True)
    peer = lax.broadcasted_iota(jnp.int32, (peers, blocks), 0).astype(jnp.float32)
    return [
        ((peer == target) & (rank == float(slot))).astype(jnp.float32) for slot in range(SLOTS)
    ]


def row_copy(peers, me, step, send_ref, recv_ref, send_sems, recv_sems):
    peer = lax.rem(me + step, peers)
    return pltpu.make_async_remote_copy(
        src_ref=send_ref.at[peer],
        dst_ref=recv_ref.at[me],
        send_sem=send_sems.at[step],
        recv_sem=recv_sems.at[step],
        device_id=(lax.axis_index("dp"), peer),
        device_id_type=MESH,
    )


def vmem(count):
    return [pl.BlockSpec(memory_space=pltpu.VMEM)] * count


NT = (((1,), (1,)), ((), ()))
ONES = 16
EARLY = 6


def dot(left, right, dims=(((1,), (0,)), ((), ()))):
    return lax.dot_general(left, right, dims, preferred_element_type=jnp.float32)


def exact_dot(left, right, dims=(((1,), (0,)), ((), ()))):
    return lax.dot_general(left, right, dims, precision=EXACT, preferred_element_type=jnp.float32)


def column_of(row):
    width = row.shape[1]
    return jnp.broadcast_to(row, (width, width)).T[:, 0:1]


def shift_rows(block):
    wide = block.astype(jnp.float32)
    columns = wide.shape[2]
    place = lax.broadcasted_iota(jnp.int32, wide.shape, 2)
    left = jnp.where(place == 0, 0.0, pltpu.roll(wide, 1, 2))
    right = jnp.where(place == columns - 1, 0.0, pltpu.roll(wide, columns - 1, 2))
    return jnp.concatenate([left.astype(jnp.bfloat16), block, right.astype(jnp.bfloat16)], axis=1)


def step_kernel(
    peers, ways, count_all, pools,
    x_ref, frac_ref, mask_ref, owners_ref, targets_ref,
    conv_ref, conv_bias_ref, mix_ref, mix_bias_ref, out_ref, out_bias_ref,
    sum_ref, coarse_ref,
    shifted, stacked, hidden_one, hidden_two, slope_one, slope_two, gain,
    row_buf, conv_acc, mix_acc, out_acc, bias_acc, sums_acc, weight_acc, flat,
    square_acc, conv_tr, mix_tr, out_tr, out_wr, picks, edge, target_send, target_recv, pred_send, pred_recv, got, part, got_part, whole,
    edge_out, edge_in, target_out, target_in, pred_out, pred_in, out_sems, in_sems, own_sem
):
    me = lax.axis_index("space")
    x = lax.axis_index("dp")
    span = ways * 2
    z = me // span
    y = lax.rem(me, span) // 2
    core = lax.rem(me, 2)
    rank = x * ways + y
    deep = z * 2 + core
    rows, channels, columns = x_ref.shape
    taps, width = conv_ref.shape
    cells = SIDE * columns
    tiles = rows // SIDE
    blocks = owners_ref.shape[1]
    across = columns // SIDE
    scale = math.sqrt(count_all)

    def plane(step):
        other = lax.rem(rank + step, TURNS)
        return other, (other // ways, z * span + lax.rem(other, ways) * 2 + core)

    def line(step):
        other = lax.rem(deep + step, TURNS)
        return other, (x, (other // 2) * span + y * 2 + lax.rem(other, 2))

    barrier = pltpu.get_barrier_semaphore()

    def greet(step, carry):
        pl.semaphore_signal(barrier, inc=1, device_id=(x, lax.rem(me + step, peers)), device_id_type=MESH)
        return carry

    def greet_plane(step, carry):
        pl.semaphore_signal(barrier, inc=1, device_id=plane(step)[1], device_id_type=MESH)
        return carry

    lax.fori_loop(1, peers, greet, 0)
    lax.fori_loop(1, TURNS, greet_plane, 0)

    owner = owner_picks(owners_ref[...], me, blocks)
    strip = strip_picks(owners_ref[pl.ds(me, 1), :], peers, blocks)
    for slot in range(SLOTS):
        picks[slot] = strip[slot]
        picks[SLOTS + slot] = owner[slot]
    sums_acc[...] = jnp.zeros_like(sums_acc)
    sums_acc[0:pools, :] = targets_ref[:, 0, :]
    target_send[:, 0, :] = pack(sums_acc[...], owner)

    def shift_some(step, carry):
        shifted[pl.ds(step * SIDE + 1, SIDE)] = shift_rows(x_ref[pl.ds(step * SIDE, SIDE)])
        return carry

    lax.fori_loop(0, tiles, shift_some, 0)

    def fill_ones(step, carry):
        stacked[step, taps : taps + ONES, :] = jnp.ones((ONES, cells), jnp.bfloat16)
        hidden_one[step, width : width + ONES, :] = jnp.ones((ONES, cells), jnp.bfloat16)
        return carry

    lax.fori_loop(0, tiles, fill_ones, 0)

    conv_t = conv_ref[...].astype(jnp.float32).T.astype(jnp.bfloat16)
    mix = mix_ref[...]
    mix_t = mix.astype(jnp.float32).T.astype(jnp.bfloat16)
    row_buf[...] = jnp.zeros_like(row_buf)
    row_buf[0:pools, :] = out_ref[...].astype(jnp.float32)
    out_wide = row_buf[...]
    out_t = out_wide[0:LANES].astype(jnp.bfloat16)
    out_w = out_wide.T[:, 0:LANES].astype(jnp.bfloat16)
    row_buf[...] = jnp.zeros_like(row_buf)
    row_buf[0:1, 0:pools] = out_bias_ref[...]
    conv_bias = column_of(conv_bias_ref[...])
    mix_bias = column_of(mix_bias_ref[...])
    out_bias = column_of(row_buf[0:1, :])[0:LANES]

    conv_tr[...] = conv_t
    mix_tr[...] = mix_t
    out_tr[...] = out_t
    out_wr[...] = out_w
    conv_acc[...] = jnp.zeros_like(conv_acc)
    mix_acc[...] = jnp.zeros_like(mix_acc)
    out_acc[...] = jnp.zeros_like(out_acc)
    bias_acc[...] = jnp.zeros_like(bias_acc)
    sums_acc[...] = jnp.zeros_like(sums_acc)
    weight_acc[...] = jnp.zeros_like(weight_acc)

    def members(step):
        column = lax.broadcasted_iota(jnp.int32, (columns, blocks), 0)
        first = (lax.broadcasted_iota(jnp.int32, (columns, blocks), 1) - step * across) * SIDE
        return ((column >= first) & (column < first + SIDE)).astype(jnp.float32)

    def forward(step, carry):
        base = step * SIDE
        for turn in range(SIDE):
            window = shifted[pl.ds(base + turn, 3)]
            stacked[step, 0:taps, turn * columns : (turn + 1) * columns] = window.reshape(taps, columns)
        pre_one = dot(conv_tr[...], stacked[step, 0:taps, :]) + conv_bias
        value_one, slope = gelu_pair(pre_one)
        slope_one[step] = slope
        narrow = value_one.astype(jnp.bfloat16)
        hidden_one[step, 0:width, :] = narrow
        pre_two = dot(mix_tr[...], narrow) + mix_bias
        value_two, slope = gelu_pair(pre_two)
        slope_two[step] = slope
        narrow = value_two.astype(jnp.bfloat16)
        hidden_two[step] = narrow
        raw = dot(out_tr[...], narrow) + out_bias
        window = pl.ds(pl.multiple_of(base, SIDE), SIDE)
        weight = frac_ref[window, :] * mask_ref[window, :].astype(jnp.float32)
        weight_row = jnp.concatenate([weight[turn : turn + 1] for turn in range(SIDE)], axis=1)
        density = (jnp.maximum(raw, 0.0) + jnp.log1p(jnp.exp(-jnp.abs(raw)))) * weight_row
        gain[step] = weight_row * jax.nn.sigmoid(raw)
        folded = density[:, 0:columns]
        for turn in range(1, SIDE):
            folded = folded + density[:, turn * columns : (turn + 1) * columns]
        member = members(step)
        sums_acc[...] += exact_dot(folded, member)
        weight_acc[...] += exact_dot(
            jnp.broadcast_to(jnp.sum(weight, axis=0, keepdims=True), (SIDE, columns)), member
        )
        return carry

    def edge_copy(side):
        peer = lax.rem(me + (1 if side == 0 else peers - 1), peers)
        return pltpu.make_async_remote_copy(
            src_ref=x_ref.at[rows - 1 if side == 0 else 0],
            dst_ref=edge.at[side],
            send_sem=edge_out.at[side],
            recv_sem=edge_in.at[side],
            device_id=(x, peer),
            device_id_type=MESH,
        )

    def routed(send, recv, outs, ins):
        def begin(step, carry):
            row_copy(peers, me, step, send, recv, outs, ins).start()
            return carry

        def finish(step, carry):
            row_copy(peers, me, step, send, recv, outs, ins).wait()
            return carry

        return (
            lambda: lax.fori_loop(1, peers, begin, 0),
            lambda: lax.fori_loop(1, peers, finish, 0),
        )

    start_targets, wait_targets = routed(target_send, target_recv, target_out, target_in)
    start_pred, wait_pred = routed(pred_send, pred_recv, pred_out, pred_in)

    lax.fori_loop(1, EARLY, forward, 0)
    pl.semaphore_wait(barrier, peers - 1 + TURNS - 1)
    for side in range(2):
        edge_copy(side).start()
    start_targets()
    target_recv[pl.ds(me, 1)] = target_send[pl.ds(me, 1)]
    lax.fori_loop(EARLY, tiles - 1, forward, 0)
    for side in range(2):
        edge_copy(side).wait()
    keep_above = jnp.where(me == 0, 0.0, 1.0)
    keep_below = jnp.where(me == peers - 1, 0.0, 1.0)
    edges = edge[...].astype(jnp.float32)
    shifted[0:1] = shift_rows((edges[0:1] * keep_above).astype(jnp.bfloat16))
    shifted[rows + 1 : rows + 2] = shift_rows((edges[1:2] * keep_below).astype(jnp.bfloat16))
    lax.fori_loop(0, 2, lambda turn, carry: forward(turn * (tiles - 1), carry), 0)

    wait_targets()

    @pl.when(me >= 0)
    def _():
        denom = jnp.maximum(weight_acc[0:1, :], 1.0)
        pred = sums_acc[...] / denom
        pred_send[:, 0, :] = pack(pred, [picks[slot] for slot in range(SLOTS)])
        here = unpack(target_recv[:, 0, :], [picks[slot] for slot in range(SLOTS)])
        pool = lax.broadcasted_iota(jnp.int32, pred.shape, 0)
        residual = jnp.where(pool < pools, pred - here, 0.0)
        square_acc[...] = jnp.broadcast_to(jnp.sum(jnp.sum(residual * residual, axis=1, keepdims=True), axis=0, keepdims=True), square_acc.shape)
        sums_acc[...] = residual / (scale * denom)

    start_pred()
    pred_recv[pl.ds(me, 1)] = pred_send[pl.ds(me, 1)]

    def backward(step, carry):
        d_columns = exact_dot(sums_acc[...], members(step), NT)
        d_raw = (jnp.concatenate([d_columns] * SIDE, axis=1) * gain[step]).astype(jnp.bfloat16)
        d_wide = d_raw.astype(jnp.float32)
        bias_sum = d_wide[:, 0:columns]
        for turn in range(1, SIDE):
            bias_sum = bias_sum + d_wide[:, turn * columns : (turn + 1) * columns]
        bias_acc[...] += bias_sum
        out_acc[...] += dot(d_raw, hidden_two[step], NT)
        d_two = (dot(out_wr[...], d_raw) * slope_two[step]).astype(jnp.bfloat16)
        mix_acc[...] += dot(hidden_one[step], d_two, NT)
        d_one = (dot(mix_ref[...], d_two) * slope_one[step]).astype(jnp.bfloat16)
        conv_acc[...] += dot(stacked[step], d_one, NT)
        return carry

    lax.fori_loop(0, tiles, backward, 0)

    row_buf[...] = jnp.zeros_like(row_buf)
    row_buf[0:LANES, :] = bias_acc[...]
    out_bias_row = exact_dot(jnp.ones((SIDE, columns), jnp.float32), row_buf[...], NT)[0:1]
    base = taps + width + LANES
    flat[base:, :] = jnp.zeros((TURNS * LINES - base, width), jnp.float32)
    flat[base : base + 1, :] = conv_acc[taps : taps + 1]
    flat[base + 1 : base + 2, :] = mix_acc[width : width + 1]
    flat[base + 2 : base + 3, :] = out_bias_row
    flat[base + 3 : base + 4, :] = square_acc[0:1]
    flat[0:taps, :] = conv_acc[0:taps]
    flat[taps : taps + width, :] = mix_acc[0:width]
    flat[taps + width : base, :] = out_acc[...]

    def lines(index):
        return pl.ds(pl.multiple_of(index * LINES, LINES), LINES)

    def remote(src, dst, phase, step, device):
        return pltpu.make_async_remote_copy(
            src_ref=src,
            dst_ref=dst,
            send_sem=out_sems.at[phase, step],
            recv_sem=in_sems.at[phase, step],
            device_id=device,
            device_id_type=MESH,
        )

    def scatter_plane(step):
        other, device = plane(step)
        return remote(flat.at[lines(other)], got.at[step - 1], 0, step, device)

    def scatter_line(step):
        other, device = line(step)
        return remote(part.at[other], got_part.at[step - 1], 1, step, device)

    def gather_line(step):
        return remote(whole.at[deep], whole.at[deep], 2, step, line(step)[1])

    def gather_plane(step):
        return remote(sum_ref.at[rank], sum_ref.at[rank], 3, step, plane(step)[1])

    def start_all(build):
        def body(step, carry):
            build(step).start()
            return carry

        lax.fori_loop(1, TURNS, body, 0)

    def wait_all(build):
        def body(step, carry):
            build(step).wait()
            return carry

        lax.fori_loop(1, TURNS, body, 0)

    start_all(scatter_plane)
    wait_pred()
    coarse_ref[...] = unpack(pred_recv[:, 0, :], [picks[SLOTS + slot] for slot in range(SLOTS)])
    wait_all(scatter_plane)
    total = flat[lines(rank), :]
    for step in range(TURNS - 1):
        total = total + got[step]
    for turn in range(TURNS):
        part[turn] = total[PART * turn : PART * (turn + 1)]
    start_all(scatter_line)
    wait_all(scatter_line)
    piece = part[deep]
    for step in range(TURNS - 1):
        piece = piece + got_part[step]
    whole[deep] = piece
    start_all(gather_line)
    wait_all(gather_line)
    own = pltpu.make_async_copy(whole, sum_ref.at[rank], own_sem)
    own.start()
    own.wait()
    start_all(gather_plane)
    wait_all(gather_plane)


def run_step(
    peers, count_all, pools, x, frac, mask, owners, targets, conv, conv_bias, mix, mix_bias, out, out_bias
):
    rows, channels, columns = x.shape
    taps, width = conv.shape
    blocks = owners.shape[1]
    tiles = rows // SIDE
    cells = SIDE * columns
    f32, bf16 = jnp.float32, jnp.bfloat16
    return pl.pallas_call(
        functools.partial(step_kernel, peers, lax.axis_size("dp"), count_all, pools),
        out_shape=(
            jax.ShapeDtypeStruct((TURNS, TURNS, PART, width), f32),
            jax.ShapeDtypeStruct((LANES, blocks), f32),
        ),
        in_specs=vmem(11),
        out_specs=tuple(vmem(2)),
        scratch_shapes=[
            pltpu.VMEM((rows + 2, 3 * channels, columns), bf16),
            pltpu.VMEM((tiles, taps + ONES, cells), bf16),
            pltpu.VMEM((tiles, width + ONES, cells), bf16),
            pltpu.VMEM((tiles, width, cells), bf16),
            pltpu.VMEM((tiles, width, cells), f32),
            pltpu.VMEM((tiles, width, cells), f32),
            pltpu.VMEM((tiles, LANES, cells), f32),
            pltpu.VMEM((width, columns), f32),
            pltpu.VMEM((taps + ONES, width), f32),
            pltpu.VMEM((width + ONES, width), f32),
            pltpu.VMEM((LANES, width), f32),
            pltpu.VMEM((LANES, columns), f32),
            pltpu.VMEM((LANES, blocks), f32),
            pltpu.VMEM((SIDE, blocks), f32),
            pltpu.VMEM((TURNS * LINES, width), f32),
            pltpu.VMEM((SIDE, width), f32),
            pltpu.VMEM((width, taps), bf16),
            pltpu.VMEM((width, width), bf16),
            pltpu.VMEM((LANES, width), bf16),
            pltpu.VMEM((width, LANES), bf16),
            pltpu.VMEM((2 * SLOTS, peers, blocks), f32),
            pltpu.VMEM((2, channels, columns), bf16),
            pltpu.VMEM((peers, 1, 128), f32),
            pltpu.VMEM((peers, 1, 128), f32),
            pltpu.VMEM((peers, 1, 128), f32),
            pltpu.VMEM((peers, 1, 128), f32),
            pltpu.VMEM((TURNS - 1, LINES, width), f32),
            pltpu.VMEM((TURNS, PART, width), f32),
            pltpu.VMEM((TURNS - 1, PART, width), f32),
            pltpu.VMEM((TURNS, PART, width), f32),
            pltpu.SemaphoreType.DMA((2,)),
            pltpu.SemaphoreType.DMA((2,)),
            pltpu.SemaphoreType.DMA((peers,)),
            pltpu.SemaphoreType.DMA((peers,)),
            pltpu.SemaphoreType.DMA((peers,)),
            pltpu.SemaphoreType.DMA((peers,)),
            pltpu.SemaphoreType.DMA((4, TURNS)),
            pltpu.SemaphoreType.DMA((4, TURNS)),
            pltpu.SemaphoreType.DMA,
        ],
        compiler_params=pltpu.CompilerParams(collective_id=0, has_side_effects=True),
        name="train_step",
    )(x, frac, mask, owners, targets, conv, conv_bias, mix, mix_bias, out, out_bias)


def finish_kernel(
    count_all, pools, sum_ref, coarse_ref,
    pred_out, conv_out, conv_bias_out, mix_out, mix_bias_out, out_out, out_bias_out, loss_out
):
    taps = conv_out.shape[0]
    width = mix_out.shape[0]
    for turn in range(TURNS):
        lines = sum_ref[turn].reshape(LINES, width)
        first = turn * LINES
        if first < taps:
            conv_out[first : first + LINES, :] = lines
        elif first < taps + width:
            mix_out[first - taps : first - taps + LINES, :] = lines
        elif first == taps + width:
            out_out[...] = lines[0:pools]
            conv_bias_out[...] = lines[LANES : LANES + 1]
            mix_bias_out[...] = lines[LANES + 1 : LANES + 2]
            out_bias_out[...] = lines[LANES + 2 : LANES + 3, 0:pools]
            loss_out[...] = 0.5 * lines[LANES + 3 : LANES + 4, 0:1] / count_all
    pred_out[:, 0, :] = coarse_ref[0:pools, :]


def finish(count_all, pools, taps, summed, coarse):
    width = summed.shape[-1]
    shapes = [
        (pools, 1, coarse.shape[1]), (taps, width), (1, width), (width, width), (1, width), (pools, width),
        (1, pools), (1, 1),
    ]
    return pl.pallas_call(
        functools.partial(finish_kernel, count_all, pools),
        out_shape=tuple(jax.ShapeDtypeStruct(shape, jnp.float32) for shape in shapes),
        in_specs=vmem(2),
        out_specs=tuple(vmem(len(shapes))),
        name="finish",
    )(summed, coarse)


def on_device(
    fields,
    land_mask,
    land_frac,
    owner_map,
    targets,
    conv_weight,
    conv_bias,
    mix_weight,
    mix_bias,
    out_weight,
    out_bias,
):
    peers = lax.axis_size("space")
    pools = out_weight.shape[1]
    width = conv_bias.shape[0]
    blocks = fields.shape[2] // SIDE * (fields.shape[3] // SIDE)
    count_all = lax.axis_size("dp") * pools * owner_map.shape[0]
    x = fields[0].transpose(1, 0, 2)
    conv = conv_weight.reshape(-1, width)
    summed, coarse = run_step(
        peers, count_all, pools, x, land_frac, land_mask, owner_map.reshape(peers, blocks),
        targets.transpose(1, 0, 2), conv, conv_bias[None], mix_weight, mix_bias[None],
        out_weight.T, out_bias[None],
    )
    pred_out, conv_out, conv_bias_out, mix_out, mix_bias_out, out_out, out_bias_out, loss = finish(
        count_all, pools, conv.shape[0], summed, coarse
    )
    return (
        pred_out.transpose(1, 0, 2),
        conv_out.reshape(conv_weight.shape),
        conv_bias_out[0],
        mix_out,
        mix_bias_out[0],
        out_out.T,
        out_bias_out[0],
        loss[0, 0],
    )


def solution(mesh):
    placed = (
        P("dp", None, "space", None),
        P("space", None),
        P("space", None),
        P(),
        P("dp", None, "space"),
        P(),
        P(),
        P(),
        P(),
        P(),
        P(),
    )
    return jax.shard_map(
        on_device,
        mesh=mesh,
        in_specs=placed,
        out_specs=(P("dp", None, "space"), P(), P(), P(), P(), P(), P(), P()),
        check_vma=False,
    )
```

time: 96.1 us -> 76 us (0.79)
  Pallas kernels: 83.1 us -> 71.3 us
  starting transfers between devices: 7.2 us -> 0 us
    pallas_call x3 -> x1, Pallas kernels: 81.4 us -> 69.6 us  [run_step(): pl.pallas_call(functools.partial(step_kernel, peers, lax.axis_size('dp'),...]
    ppermute x2 -> x0, starting transfers between devices: 7.2 us -> none  [the longest x1 5.28 us: halo_rows(): below = lax.ppermute(block[:1], 'space', backward)]
    unnamed x13 -> x1, local copies, waits for them, and re-layouts: 3.99 us -> 2.32 us
  transfers between devices with their start and end apart: 2 -> 0, of which waited for: 0 -> 0; matrix products, arithmetic and copies ran while one was open for 1% -> 0% of each run, Pallas kernels for 19% -> 0%
where the time goes in v2:
time: 76 us; the launch traced here: 75.8 us
  Pallas kernels  71.3 us (94%)
  local copies, waits for them, and re-layouts  3.82 us (5%)
    pallas_call x1, Pallas kernels, run_step(): pl.pallas_call(functools.partial(step_kernel, peers, lax.axis_size('dp'),...  69.6 us
    unnamed x1, local copies, waits for them, and re-layouts  2.32 us
    pallas_call x1, Pallas kernels, finish(): pl.pallas_call(functools.partial(finish_kernel, count_all, pools), out_sh...  1.7 us

profile of v2, /device:TPU:1, one launch (start us, length us, event | category | flops | bytes accessed | tf_op | source)
XLA Modules:
  0.0 75.8 jit_solution(12906709998615949472)
XLA Ops:
  0.6 1.5 %reshape.25.owners_ref = s32[64,192]{1,0:T(8,128)} reshape(s32[12288]{0:T(1024)} %param.14) | data formatting | bytes 98304 | tf_op jit(solution)/shard_map/reshape | solution.py:539
  2.1 2.3 %copy.21 = bf16[1,32,96,128]{3,1,2,0:T(8,128)(2,1)} copy(bf16[1,32,96,128]{3,2,1,0:T(8,128)(2,1)} %param.11) | data formatting | bytes 1572864 | tf_op args[0]
  4.5 69.6 %train_step.1 = (f32[16,16,2,128]{3,2,1,0:T(2,128)}, f32[16,192]{1,0:T(8,128)}) custom-call(bf16[96,32,128]{2,1,0:T(8,128)(2,1)} %bitcast.18, f32[96,128]{1,0:T(8,128)} %frac_ref.1, s32[96,128]{1,0:T(8,128)} %mask_ref.1, s32[64,192]{1,0:T(8,128)} %reshape.25.owners_ref, f32[14,1,192]{2,1,0:T(1,128)} %bitcast.20, bf16[288,128]{1,0:T(8,128)(2,1)} %bitcast.19, ...), custom_call_target="tpu_custom_call" | custom-call | tf_op jit(solution)/shard_map/train_step/pallas_call | solution.py:427
  74.1 1.7 %finish.1 = (f32[14,1,192]{2,1,0:T(1,128)}, f32[288,128]{1,0:T(8,128)}, f32[1,128]{1,0:T(1,128)}, f32[128,128]{1,0:T(8,128)}, f32[1,128]{1,0:T(1,128)}, /*index=...) custom-call(f32[16,16,2,128]{3,2,1,0:T(2,128)} %get-tuple-element.18.sum_ref, f32[16,192]{1,0:T(8,128)} %get-tuple-element.19.coarse_ref), custom_call_target="tpu_custom_call" | custom-call | tf_op jit(solution)/shard_map/finish/pallas_call | solution.py:509

commit v3 on v2

--- a/solution.py
+++ b/solution.py
@@ -16,13 +16,10 @@
 
 
 def gelu_pair(pre):
-    inner = ROOT_TWO_PI * (pre + CUBIC * pre * pre * pre)
-    tanh_value = jnp.tanh(inner)
-    value = 0.5 * pre * (1.0 + tanh_value)
-    slope = 0.5 * (1.0 + tanh_value) + 0.5 * pre * (1.0 - tanh_value * tanh_value) * ROOT_TWO_PI * (
-        1.0 + 3.0 * CUBIC * pre * pre
-    )
-    return (value, slope)
+    square = pre * pre
+    gate = 0.5 + 0.5 * jnp.tanh(pre * (ROOT_TWO_PI + ROOT_TWO_PI * CUBIC * square))
+    rate = 2.0 * ROOT_TWO_PI + 6.0 * ROOT_TWO_PI * CUBIC * square
+    return (pre * gate, gate + pre * rate * (gate - gate * gate))
 
 
 MESH = pl.DeviceIdType.MESH
@@ -119,6 +116,16 @@
 def column_of(row):
     width = row.shape[1]
     return jnp.broadcast_to(row, (width, width)).T[:, 0:1]
+
+
+def bias_parts(column):
+    high = column.astype(jnp.bfloat16).astype(jnp.float32)
+    rest = column - high
+    middle = rest.astype(jnp.bfloat16).astype(jnp.float32)
+    low = rest - middle
+    lane = lax.broadcasted_iota(jnp.int32, (column.shape[0], ONES), 1)
+    parts = jnp.where(lane == 0, high, jnp.where(lane == 1, middle, jnp.where(lane == 2, low, 0.0)))
+    return parts.astype(jnp.bfloat16)
 
 
 def shift_rows(block):
@@ -213,8 +220,10 @@
     mix_bias = column_of(mix_bias_ref[...])
     out_bias = column_of(row_buf[0:1, :])[0:LANES]
 
-    conv_tr[...] = conv_t
-    mix_tr[...] = mix_t
+    conv_tr[:, 0:taps] = conv_t
+    conv_tr[:, taps : taps + ONES] = bias_parts(conv_bias)
+    mix_tr[:, 0:width] = mix_t
+    mix_tr[:, width : width + ONES] = bias_parts(mix_bias)
     out_tr[...] = out_t
     out_wr[...] = out_w
     conv_acc[...] = jnp.zeros_like(conv_acc)
@@ -234,12 +243,11 @@
         for turn in range(SIDE):
             window = shifted[pl.ds(base + turn, 3)]
             stacked[step, 0:taps, turn * columns : (turn + 1) * columns] = window.reshape(taps, columns)
-        pre_one = dot(conv_tr[...], stacked[step, 0:taps, :]) + conv_bias
+        pre_one = dot(conv_tr[...], stacked[step])
         value_one, slope = gelu_pair(pre_one)
         slope_one[step] = slope
-        narrow = value_one.astype(jnp.bfloat16)
-        hidden_one[step, 0:width, :] = narrow
-        pre_two = dot(mix_tr[...], narrow) + mix_bias
+        hidden_one[step, 0:width, :] = value_one.astype(jnp.bfloat16)
+        pre_two = dot(mix_tr[...], hidden_one[step])
         value_two, slope = gelu_pair(pre_two)
         slope_two[step] = slope
         narrow = value_two.astype(jnp.bfloat16)
@@ -449,8 +457,8 @@
             pltpu.VMEM((SIDE, blocks), f32),
             pltpu.VMEM((TURNS * LINES, width), f32),
             pltpu.VMEM((SIDE, width), f32),
-            pltpu.VMEM((width, taps), bf16),
-            pltpu.VMEM((width, width), bf16),
+            pltpu.VMEM((width, taps + ONES), bf16),
+            pltpu.VMEM((width, width + ONES), bf16),
             pltpu.VMEM((LANES, width), bf16),
             pltpu.VMEM((width, LANES), bf16),
             pltpu.VMEM((2 * SLOTS, peers, blocks), f32),

time: 76 us -> 73.5 us (0.967)
  Pallas kernels: 71.3 us -> 68.8 us
    pallas_call x1, Pallas kernels: 69.6 us -> 67.1 us  [run_step(): pl.pallas_call(functools.partial(step_kernel, peers, lax.axis_size('dp'),...]
where the time goes in v3:
time: 73.5 us; the launch traced here: 73.3 us
  Pallas kernels  68.8 us (94%)
  local copies, waits for them, and re-layouts  3.82 us (5%)
    pallas_call x1, Pallas kernels, run_step(): pl.pallas_call(functools.partial(step_kernel, peers, lax.axis_size('dp'),...  67.1 us
    unnamed x1, local copies, waits for them, and re-layouts  2.32 us
    pallas_call x1, Pallas kernels, finish(): pl.pallas_call(functools.partial(finish_kernel, count_all, pools), out_sh...  1.7 us
    reshape x1, local copies, waits for them, and re-layouts, on_device(): owner_map.reshape(peers, blocks)  1.5 us

profile of v3, /device:TPU:1, one launch (start us, length us, event | category | flops | bytes accessed | tf_op | source)
XLA Modules:
  0.0 73.3 jit_solution(14022893457080730067)
XLA Ops:
  0.6 1.5 %reshape.25.owners_ref = s32[64,192]{1,0:T(8,128)} reshape(s32[12288]{0:T(1024)} %param.14) | data formatting | bytes 98304 | tf_op jit(solution)/shard_map/reshape | solution.py:547
  2.1 2.3 %copy.21 = bf16[1,32,96,128]{3,1,2,0:T(8,128)(2,1)} copy(bf16[1,32,96,128]{3,2,1,0:T(8,128)(2,1)} %param.11) | data formatting | bytes 1572864 | tf_op args[0]
  4.5 67.1 %train_step.1 = (f32[16,16,2,128]{3,2,1,0:T(2,128)}, f32[16,192]{1,0:T(8,128)}) custom-call(bf16[96,32,128]{2,1,0:T(8,128)(2,1)} %bitcast.18, f32[96,128]{1,0:T(8,128)} %frac_ref.1, s32[96,128]{1,0:T(8,128)} %mask_ref.1, s32[64,192]{1,0:T(8,128)} %reshape.25.owners_ref, f32[14,1,192]{2,1,0:T(1,128)} %bitcast.20, bf16[288,128]{1,0:T(8,128)(2,1)} %bitcast.19, ...), custom_call_target="tpu_custom_call" | custom-call | tf_op jit(solution)/shard_map/train_step/pallas_call | solution.py:435
  71.6 1.7 %finish.1 = (f32[14,1,192]{2,1,0:T(1,128)}, f32[288,128]{1,0:T(8,128)}, f32[1,128]{1,0:T(1,128)}, f32[128,128]{1,0:T(8,128)}, f32[1,128]{1,0:T(1,128)}, /*index=...) custom-call(f32[16,16,2,128]{3,2,1,0:T(2,128)} %get-tuple-element.18.sum_ref, f32[16,192]{1,0:T(8,128)} %get-tuple-element.19.coarse_ref), custom_call_target="tpu_custom_call" | custom-call | tf_op jit(solution)/shard_map/finish/pallas_call | solution.py:517

commit v4 on v3

--- a/solution.py
+++ b/solution.py
@@ -118,6 +118,20 @@
     return jnp.broadcast_to(row, (width, width)).T[:, 0:1]
 
 
+def regroup(rows_ref, out_ref):
+    half = out_ref.shape[0] // 2
+    first, middle, last = (rows_ref[pl.ds(start, half, 3), :] for start in range(3))
+    middle_turned = pltpu.roll(middle, 64, 1)
+    last_turned = pltpu.roll(last, 64, 1)
+    lane = lax.broadcasted_iota(jnp.int32, first.shape, 1)
+    mixed = jnp.where(lane < 64, middle_turned, last_turned)
+    for turn in range(half):
+        out_ref[2 * turn : 2 * turn + 1, 0:128] = first[turn : turn + 1]
+        out_ref[2 * turn : 2 * turn + 1, 128:192] = middle[turn : turn + 1, 0:64]
+        out_ref[2 * turn + 1 : 2 * turn + 2, 0:128] = mixed[turn : turn + 1]
+        out_ref[2 * turn + 1 : 2 * turn + 2, 128:192] = last_turned[turn : turn + 1, 0:64]
+
+
 def bias_parts(column):
     high = column.astype(jnp.bfloat16).astype(jnp.float32)
     rest = column - high
@@ -139,12 +153,12 @@
 
 def step_kernel(
     peers, ways, count_all, pools,
-    x_ref, frac_ref, mask_ref, owners_ref, targets_ref,
+    x_ref, frac_ref, mask_ref, owner_rows_ref, targets_ref,
     conv_ref, conv_bias_ref, mix_ref, mix_bias_ref, out_ref, out_bias_ref,
     sum_ref, coarse_ref,
     shifted, stacked, hidden_one, hidden_two, slope_one, slope_two, gain,
     row_buf, conv_acc, mix_acc, out_acc, bias_acc, sums_acc, weight_acc, flat,
-    square_acc, conv_tr, mix_tr, out_tr, out_wr, picks, edge, target_send, target_recv, pred_send, pred_recv, got, part, got_part, whole,
+    owners_ref, square_acc, conv_tr, mix_tr, out_tr, out_wr, picks, edge, target_send, target_recv, pred_send, pred_recv, got, part, got_part, whole,
     edge_out, edge_in, target_out, target_in, pred_out, pred_in, out_sems, in_sems, own_sem
 ):
     me = lax.axis_index("space")
@@ -184,6 +198,7 @@
     lax.fori_loop(1, peers, greet, 0)
     lax.fori_loop(1, TURNS, greet_plane, 0)
 
+    regroup(owner_rows_ref, owners_ref)
     owner = owner_picks(owners_ref[...], me, blocks)
     strip = strip_picks(owners_ref[pl.ds(me, 1), :], peers, blocks)
     for slot in range(SLOTS):
@@ -428,7 +443,7 @@
 ):
     rows, channels, columns = x.shape
     taps, width = conv.shape
-    blocks = owners.shape[1]
+    blocks = owners.size // peers
     tiles = rows // SIDE
     cells = SIDE * columns
     f32, bf16 = jnp.float32, jnp.bfloat16
@@ -456,6 +471,7 @@
             pltpu.VMEM((LANES, blocks), f32),
             pltpu.VMEM((SIDE, blocks), f32),
             pltpu.VMEM((TURNS * LINES, width), f32),
+            pltpu.VMEM((peers, blocks), jnp.int32),
             pltpu.VMEM((SIDE, width), f32),
             pltpu.VMEM((width, taps + ONES), bf16),
             pltpu.VMEM((width, width + ONES), bf16),
@@ -544,7 +560,7 @@
     x = fields[0].transpose(1, 0, 2)
     conv = conv_weight.reshape(-1, width)
     summed, coarse = run_step(
-        peers, count_all, pools, x, land_frac, land_mask, owner_map.reshape(peers, blocks),
+        peers, count_all, pools, x, land_frac, land_mask, owner_map.reshape(-1, 128),
         targets.transpose(1, 0, 2), conv, conv_bias[None], mix_weight, mix_bias[None],
         out_weight.T, out_bias[None],
     )

time: 73.5 us -> 72 us (0.980)
  local copies, waits for them, and re-layouts: 3.82 us -> 2.32 us
    reshape x1 -> x0, local copies, waits for them, and re-layouts: 1.5 us -> none  [on_device(): owner_map.reshape(peers, blocks)]
where the time goes in v4:
time: 72 us; the launch traced here: 71.8 us
  Pallas kernels  68.9 us (96%)
  local copies, waits for them, and re-layouts  2.32 us (3%)
    pallas_call x1, Pallas kernels, run_step(): pl.pallas_call(functools.partial(step_kernel, peers, lax.axis_size('dp'),...  67.2 us
    unnamed x1, local copies, waits for them, and re-layouts  2.32 us
    pallas_call x1, Pallas kernels, finish(): pl.pallas_call(functools.partial(finish_kernel, count_all, pools), out_sh...  1.7 us

profile of v4, /device:TPU:1, one launch (start us, length us, event | category | flops | bytes accessed | tf_op | source)
XLA Modules:
  0.0 71.8 jit_solution(3316003263410592421)
XLA Ops:
  0.6 2.3 %copy.21 = bf16[1,32,96,128]{3,1,2,0:T(8,128)(2,1)} copy(bf16[1,32,96,128]{3,2,1,0:T(8,128)(2,1)} %param.11) | data formatting | bytes 1572864 | tf_op args[0]
  3.0 67.2 %train_step.1 = (f32[16,16,2,128]{3,2,1,0:T(2,128)}, f32[16,192]{1,0:T(8,128)}) custom-call(bf16[96,32,128]{2,1,0:T(8,128)(2,1)} %bitcast.19, f32[96,128]{1,0:T(8,128)} %frac_ref.1, s32[96,128]{1,0:T(8,128)} %mask_ref.1, s32[96,128]{1,0:T(8,128)} %bitcast.21, f32[14,1,192]{2,1,0:T(1,128)} %bitcast.22, bf16[288,128]{1,0:T(8,128)(2,1)} %bitcast.20, ...), custom_call_target="tpu_custom_call" | custom-call | tf_op jit(solution)/shard_map/train_step/pallas_call | solution.py:450
  70.1 1.7 %finish.1 = (f32[14,1,192]{2,1,0:T(1,128)}, f32[288,128]{1,0:T(8,128)}, f32[1,128]{1,0:T(1,128)}, f32[128,128]{1,0:T(8,128)}, f32[1,128]{1,0:T(1,128)}, /*index=...) custom-call(f32[16,16,2,128]{3,2,1,0:T(2,128)} %get-tuple-element.18.sum_ref, f32[16,192]{1,0:T(8,128)} %get-tuple-element.19.coarse_ref), custom_call_target="tpu_custom_call" | custom-call | tf_op jit(solution)/shard_map/finish/pallas_call | solution.py:533
